TPU v7x, 128 devices: a whole 4x4x4 slice. The times are simulated.
128 devices in a mesh: seq: 16 (over z_lo, y, core), head: 8 (over z_hi, x).
Axes of the slice: x: 4, y: 4, z: 4 (z_hi: 2, z_lo: 2; z = z_hi * 2 + z_lo), core: 2. Of those that a mesh axis runs over, the one named last changes fastest.
Arguments:
- queries: bfloat16 [8192, 4096], P('seq', 'head'), may hold values from -6 to 6
- new_keys: bfloat16 [8192, 4096], P('seq', 'head'), may hold values from -6 to 6
- new_values: bfloat16 [8192, 4096], P('seq', 'head'), may hold values from -6 to 6
- pool_keys: bfloat16 [16384, 4096], P('seq', 'head'), may hold values from -6 to 6
- pool_values: bfloat16 [16384, 4096], P('seq', 'head'), may hold values from -6 to 6
- cache_len: int32 [4], replicated, may hold values from 128 to 4096, as said below
- cached_table: int32 [4, 32], replicated, may hold values from -1 to 127, as said below
- free_blocks: int32 [4, 16], replicated, may hold values from 0 to 127, as said below
- residual_in: bfloat16 [8192, 7168], P('seq', 'head'), may hold values from -26 to 26
- out_weight: bfloat16 [4096, 7168], P('head'), may hold values from -2.390625 to 2.390625
- out_bias: float32 [7168], P('head'), may hold values from -3 to 3
- ln_gain: float32 [7168], P('head'), may hold values from 0.1 to 1.9
- ln_bias: float32 [7168], P('head'), may hold values from -3 to 3
Outputs:
- hidden: bfloat16 [8192, 7168], P('seq', 'head')
- normed: bfloat16 [8192, 7168], P('seq', 'head')
- keys_out: bfloat16 [16384, 4096], P('seq', 'head')
- values_out: bfloat16 [16384, 4096], P('seq', 'head')
Inputs may be any that keep to these rules, and one draw needn't show every extreme that they name: `cache_len`: a multiple of 128; exactly one prompt has 4096 cached positions. `cached_table`: entry [p, j] names the pool block that holds cached positions j * 128 to j * 128 + 127 of prompt p when j < cache_len[p] / 128, and is -1 otherwise; the named blocks are all different and lie anywhere in the pool. `free_blocks`: all different and never named by cached_table; block free_blocks[p, j] lies in the pool rows held by the same index of seq as token row p * 2048 + j * 128, that is free_blocks[p, j] * 128 // 1024 == (p * 2048 + j * 128) // 512.
All inputs are finite; a program needn't handle non-finite values.
Results may differ from a plain program's by a relative error of at most 0.022.
Values may be sent and summed in bfloat16 or wider, within the bound.
No kernel may reach another device: no remote copies, remote signals or barrier semaphores. Data moves between devices by JAX's collectives and lax.ppermute only.
A program may use at most 384 MiB of HBM per device.

v0:
```python
import functools

import jax
import jax.numpy as jnp
import numpy as np
from jax import lax
from jax.experimental import pallas as pl
from jax.experimental.pallas import tpu as pltpu
from jax.sharding import Mesh
from jax.sharding import PartitionSpec as P

D = 7168
HD = 128
BLOCK = 128
ROWS = 512
HALF = 256
FRESH = 4
COLS = 896
SIZES = {"zlo": 2, "yhi": 2, "ylo": 2, "core": 2, "zhi": 2, "x": 4}
SEQ = ("zlo", "yhi", "ylo", "core")
HEAD = ("zhi", "x")
SCALE2 = HD**-0.5 * 1.4426950408889634
ANY = pl.BlockSpec(memory_space=pl.ANY)
SMEM = pl.BlockSpec(memory_space=pltpu.SMEM)
VMEM = pl.BlockSpec(memory_space=pltpu.VMEM)


def move(value, flips=(), x_step=0):
    axes = tuple(flips) + (("x",) if x_step else ())
    sizes = [SIZES[a] for a in axes]
    pairs = []
    for source in range(int(np.prod(sizes))):
        place = list(np.unravel_index(source, sizes))
        for k, a in enumerate(axes):
            place[k] = (place[k] + x_step) % 4 if a == "x" else 1 - place[k]
        pairs.append((source, int(np.ravel_multi_index(place, sizes))))
    return lax.ppermute(value, axes, pairs)


RELATION = ((), ("core",), ("ylo",), ("ylo", "core"))


def places():
    z, yh, yl, c = (lax.axis_index(a) for a in SEQ)
    group_index = yl * 2 + c
    head = (yl ^ yh) * 2 + c
    return z, yh, group_index, head


def find_spare(free, spare):
    z, yh, gi, _ = places()
    prompt = z * 2 + yh
    count = jnp.int32(0)
    for lb in range(8):
        block = (prompt * 4 + gi) * 8 + lb
        taken = free[prompt, gi * FRESH] == block
        for k in range(1, FRESH):
            taken = taken | (free[prompt, gi * FRESH + k] == block)

        @pl.when(jnp.logical_not(taken) & (count < FRESH))
        def _():
            spare[count] = lb

        count = count + jnp.where(taken, 0, 1)


class Copies:
    def __init__(self, sems):
        self.sems, self.open, self.used = sems, [], 0

    def start(self, source, target):
        one = pltpu.make_async_copy(source, target, self.sems.at[self.used])
        self.used += 1
        one.start()
        self.open.append(one)
        return one

    def wait(self):
        for one in self.open:
            one.wait()
        self.open = []


def rows_of(block):
    return pl.ds(pl.multiple_of(block * BLOCK, BLOCK), BLOCK)


def cols_of(head):
    return pl.ds(pl.multiple_of(head * HD, HD), HD)


def prep_kernel(free, q, pk, pv, fq, c0, c1, cy, spare, held, held_q, sems):
    _, yh, _, head = places()
    copies = Copies(sems)
    query = pltpu.make_async_copy(q, held_q, sems.at[sems.shape[0] - 1])
    query.start()
    find_spare(free, spare)
    for s in range(FRESH):
        for kv, source in enumerate((pk, pv)):
            copies.start(source.at[rows_of(spare[s])], held.at[kv, pl.ds(s * BLOCK, BLOCK)])
    copies.wait()
    for r, out in ((1, c1), (2, cy.at[0]), (3, cy.at[1]), (0, c0)):
        for kv in range(2):
            copies.start(held.at[kv, :, cols_of(head ^ r)], out.at[kv])
    query.wait()
    for k in range(4):
        copies.start(held_q.at[:, cols_of(k ^ (2 * yh))], fq.at[k])
    copies.wait()


def prep(free, q, pk, pv):
    shape = lambda *s: jax.ShapeDtypeStruct(s, jnp.bfloat16)
    return pl.pallas_call(
        prep_kernel,
        out_shape=[shape(4, ROWS, HD)] + [shape(2, ROWS, HD)] * 2 + [shape(2, 2, ROWS, HD)],
        in_specs=[SMEM] + [ANY] * 3,
        out_specs=[ANY] * 4,
        scratch_shapes=[
            pltpu.SMEM((FRESH,), jnp.int32),
            pltpu.VMEM((2, ROWS, 512), jnp.bfloat16),
            pltpu.VMEM((ROWS, 512), jnp.bfloat16),
            pltpu.SemaphoreType.DMA((24,)),
        ],
        cost_estimate=pl.CostEstimate(flops=0, bytes_accessed=4 << 20, transcendentals=0),
        name="prep",
    )(free, q, pk, pv)


def side_kernel(
    gate, free, table, length, nk, nv, pk, pv, weight,
    cut, ko, vo, f0, f1, fy, early, mid, late, spare, wide, new, old, sems,
):
    z, yh, gi, head = places()
    core = lax.axis_index("core")
    prompt = z * 2 + yh
    copies = Copies(sems)
    reads = [
        copies.start(weight.at[:, pl.ds(pl.multiple_of((core * 4 + n) * COLS, HD), COLS)], wide.at[n])
        for n in range(4)
    ]
    for kv, source in enumerate((nk, nv)):
        copies.start(source, new.at[kv])
    find_spare(free, spare)
    for s in range(FRESH):
        for kv, source in enumerate((pk, pv)):
            copies.start(source.at[rows_of(spare[s])], old.at[kv, pl.ds(s * BLOCK, BLOCK)])

    def one(n, counts):
        block = jnp.clip(table[prompt, n], 0, 127)
        owner, place = block // 32, (block // 8) % 4
        rank = block % 8
        for k in range(FRESH):
            rank = rank - jnp.where(free[owner, place * FRESH + k] < block, 1, 0)
        rank = jnp.clip(rank, 0, FRESH - 1)
        far_y = (owner % 2) ^ yh
        group = ((owner // 2) ^ z) * 2 + far_y
        r = place ^ gi ^ (2 * far_y)
        is_late = jnp.where(group == 3, 1, 0)
        is_mid = jnp.where((group > 0) & (group < 3) & (r > 1), 1, 0)
        early[1 + counts[0]] = (
            jnp.clip(jnp.where(group == 0, r, 2 + 2 * group + r), 0, 7) * FRESH + rank
        )
        mid[1 + counts[1]] = jnp.clip(2 * group + r - 4, 0, 3) * FRESH + rank
        late[1 + counts[2]] = r * FRESH + rank
        return counts[0] + 1 - is_late - is_mid, counts[1] + is_mid, counts[2] + is_late

    counts = lax.fori_loop(0, length[prompt] // BLOCK, one, (jnp.int32(0),) * 3)
    for listed, count in zip((early, mid, late), counts):
        listed[0] = count
    copies.wait()
    for n in range(4):
        copies.start(wide.at[n], cut.at[n])
    for kv, out in enumerate((ko, vo)):
        for r, target in ((2, fy.at[0]), (3, fy.at[1]), (1, f1), (0, f0)):
            copies.start(new.at[kv, :, cols_of(head ^ r)], target.at[kv])
        for s in range(FRESH):
            rows = pl.ds(s * BLOCK, BLOCK)
            into = jnp.clip(free[prompt, gi * FRESH + s] - (prompt * 4 + gi) * 8, 0, 7)
            copies.start(new.at[kv, rows], out.at[rows_of(into)])
            copies.start(old.at[kv, rows], out.at[rows_of(spare[s])])
    copies.wait()


def side(gate, free, table, length, nk, nv, pk, pv, weight):
    shape = lambda *s: jax.ShapeDtypeStruct(s, jnp.bfloat16)
    return pl.pallas_call(
        side_kernel,
        out_shape=[shape(4, 512, COLS)]
        + [shape(1024, 512)] * 2
        + [shape(2, ROWS, HD)] * 2
        + [shape(2, 2, ROWS, HD)]
        + [jax.ShapeDtypeStruct((40,), jnp.int32)] * 3,
        in_specs=[SMEM] * 4 + [ANY] * 5,
        out_specs=[ANY] * 6 + [SMEM] * 3,
        scratch_shapes=[
            pltpu.SMEM((FRESH,), jnp.int32),
            pltpu.VMEM((4, 512, COLS), jnp.bfloat16),
            pltpu.VMEM((2, ROWS, 512), jnp.bfloat16),
            pltpu.VMEM((2, ROWS, 512), jnp.bfloat16),
            pltpu.SemaphoreType.DMA((48,)),
        ],
        cost_estimate=pl.CostEstimate(flops=0, bytes_accessed=14 << 20, transcendentals=0),
        name="side",
    )(gate, free, table, length, nk, nv, pk, pv, weight)


def softmax_step(q, k, v, state, mask=None):
    peak, total, acc = state
    s = lax.dot_general(k, q, (((1,), (1,)), ((), ())), preferred_element_type=jnp.float32)
    if mask is not None:
        width = mask.shape[1]
        parts = [jnp.where(mask, s[:, :width], -1e30)]
        if width < s.shape[1]:
            parts.append(s[:, width:])
        s = jnp.concatenate(parts, axis=1)
    new_peak = jnp.maximum(peak, jnp.max(s, axis=0, keepdims=True))
    p = jnp.exp2((s - new_peak) * SCALE2)
    fade = jnp.exp2((peak - new_peak) * SCALE2)
    total = total * fade + jnp.sum(p, axis=0, keepdims=True)
    acc = acc * fade + lax.dot_general(
        v, p.astype(jnp.bfloat16), (((0,), (0,)), ((), ())), preferred_element_type=jnp.float32
    )
    return new_peak, total, acc


def pool_steps(queries, blocks, pool, acc, row):
    count = blocks[0]

    def group(first, width, q, cols, masked):
        at = [first + m for m in range(width)]
        mask = None
        if masked:
            key = lax.broadcasted_iota(jnp.int32, (width * BLOCK, q.shape[0]), 0)
            mask = key < (count - first) * BLOCK
            at = [jnp.minimum(a, count - 1) for a in at]
        at = [blocks[1 + a] for a in at]
        k, v = (
            jnp.concatenate([pool[a // FRESH, kv, rows_of(a % FRESH), :] for a in at], axis=0)
            for kv in range(2)
        )
        state = (row[0:1, cols], row[1:2, cols], acc[:, cols])
        state = softmax_step(q, k, v, state, mask)
        row[0:1, cols] = state[0]
        row[1:2, cols] = state[1]
        acc[:, cols] = state[2]

    wide = count // 8

    def eight(n, carry):
        group(n * 8, 8, queries[...].reshape(4 * ROWS, HD), pl.ds(0, 4 * ROWS), False)
        return carry

    lax.fori_loop(0, wide, eight, 0)

    def four(n, carry):
        cols = pl.ds(pl.multiple_of((n % 4) * ROWS, ROWS), ROWS)
        group(wide * 8 + (n // 4) * 4, 4, queries[n % 4], cols, True)
        return carry

    lax.fori_loop(0, (count - wide * 8 + 3) // 4 * 4, four, 0)


STATE = [
    jax.ShapeDtypeStruct((HD, 4 * ROWS), jnp.float32),
    jax.ShapeDtypeStruct((8, 4 * ROWS), jnp.float32),
]


def early_kernel(blocks, fq, g0, g1, y0, z0, acc, row, pool, sems):
    copies = Copies(sems)
    for n, p in enumerate((g0, g1, y0, z0)):
        copies.start(p, pool.at[pl.ds(2 * n, 2)])
    row[0:1, :] = jnp.full((1, 4 * ROWS), -1e30, jnp.float32)
    row[1:2, :] = jnp.zeros((1, 4 * ROWS), jnp.float32)
    acc[...] = jnp.zeros_like(acc)
    copies.wait()
    pool_steps(fq, blocks, pool, acc, row)


def attend_early(blocks, fq, pools):
    return pl.pallas_call(
        early_kernel,
        out_shape=STATE,
        in_specs=[SMEM, VMEM] + [ANY] * 4,
        out_specs=[VMEM] * 2,
        scratch_shapes=[
            pltpu.VMEM((8, 2, ROWS, HD), jnp.bfloat16),
            pltpu.SemaphoreType.DMA((4,)),
        ],
        cost_estimate=pl.CostEstimate(
            flops=4_000_000 * 512, bytes_accessed=4 << 20, transcendentals=4_000_000
        ),
        name="attend_early",
    )(blocks, fq, *pools)


def fresh_kernel(
    blocks, fq, f0, f1, fy, f3, y1, z1, acc, row, acc_out, row_out, fresh, pool, sems
):
    _, _, gi, _ = places()
    copies = [
        pltpu.make_async_copy(f, fresh.at[gi ^ r], sems.at[r])
        for r, f in enumerate((f0, f1, fy.at[0], f3))
    ] + [
        pltpu.make_async_copy(p, pool.at[pl.ds(2 * n, 2)], sems.at[4 + n])
        for n, p in enumerate((y1, z1))
    ]
    for one in copies:
        one.start()
    acc_out[...] = acc[...]
    row_out[...] = row[...]
    for one in copies:
        one.wait()
    for k in range(4):
        n = (4 - k) * ROWS
        cols = pl.ds(k * ROWS, n)
        key = lax.broadcasted_iota(jnp.int32, (ROWS, ROWS), 0)
        query = lax.broadcasted_iota(jnp.int32, (ROWS, ROWS), 1)
        state = (row_out[0:1, cols], row_out[1:2, cols], acc_out[:, cols])
        q = fq[k:].reshape(n, HD)
        state = softmax_step(q, fresh[k, 0], fresh[k, 1], state, key <= query)
        row_out[0:1, cols] = state[0]
        row_out[1:2, cols] = state[1]
        acc_out[:, cols] = state[2]
    pool_steps(fq, blocks, pool, acc_out, row_out)


def attend_fresh(blocks, fq, fresh, pools, acc, row):
    return pl.pallas_call(
        fresh_kernel,
        out_shape=STATE,
        in_specs=[SMEM, VMEM] + [ANY] * 6 + [VMEM] * 2,
        out_specs=[VMEM] * 2,
        scratch_shapes=[
            pltpu.VMEM((4, 2, ROWS, HD), jnp.bfloat16),
            pltpu.VMEM((4, 2, ROWS, HD), jnp.bfloat16),
            pltpu.SemaphoreType.DMA((6,)),
        ],
        cost_estimate=pl.CostEstimate(
            flops=2_600_000 * 512, bytes_accessed=4 << 20, transcendentals=2_600_000
        ),
        name="attend_fresh",
    )(blocks, fq, *fresh, *pools, acc, row)


def late_kernel(
    blocks, fq, d0, d1, acc, row, o0, o1, o2, o3, out1, pool, mixed, rows, sems
):
    _, _, gi, _ = places()
    copies = [
        pltpu.make_async_copy(p, pool.at[pl.ds(2 * n, 2)], sems.at[n])
        for n, p in enumerate((d0, d1))
    ]
    for one in copies:
        one.start()
    for one in copies:
        one.wait()
    mixed[...] = acc[...]
    rows[...] = row[...]
    pool_steps(fq, blocks, pool, mixed, rows)
    mixed[...] = mixed[...] / rows[1:2, :]
    for r, out in enumerate((o0, o1, o2, o3)):
        cols = pl.ds(pl.multiple_of((gi ^ r) * ROWS, ROWS), HALF)
        out[...] = mixed[:, cols].astype(jnp.bfloat16).T
    for k in range(4):
        out1[k] = mixed[:, pl.ds(k * ROWS + HALF, HALF)].astype(jnp.bfloat16).T


def attend_late(blocks, fq, pools, acc, row):
    return pl.pallas_call(
        late_kernel,
        out_shape=[jax.ShapeDtypeStruct((HALF, HD), jnp.bfloat16)] * 4
        + [jax.ShapeDtypeStruct((4, HALF, HD), jnp.bfloat16)],
        in_specs=[SMEM, VMEM] + [ANY] * 2 + [VMEM] * 2,
        out_specs=[VMEM] * 5,
        scratch_shapes=[
            pltpu.VMEM((4, 2, ROWS, HD), jnp.bfloat16),
            pltpu.VMEM((HD, 4 * ROWS), jnp.float32),
            pltpu.VMEM((8, 4 * ROWS), jnp.float32),
            pltpu.SemaphoreType.DMA((2,)),
        ],
        cost_estimate=pl.CostEstimate(
            flops=2_000_000 * 512, bytes_accessed=4 << 20, transcendentals=2_000_000
        ),
        name="attend_late",
    )(blocks, fq, *pools, acc, row)


def project_kernel(far, ordered, a0, ap, am, a2a, a2b, mine, other, out, at, wt, sems):
    core = lax.axis_index("core")
    _, yh, _, head = places()
    head = 2 * yh if ordered else head
    x = lax.axis_index("x")
    half = lax.axis_index("zhi") ^ far
    copies = Copies(sems)
    for source, step, k0 in ((a0, 0, 0), (ap, 3, 0), (am, 1, 0), (a2a, 2, 0), (a2b, 2, 2)):
        for k in range(source.shape[0]):
            col = ((x + step) % 4) * 512 + (head ^ (k0 + k)) * HD
            copies.start(source.at[k], at.at[:, pl.ds(pl.multiple_of(col, HD), HD)])
    parts = (slice(0, 512), slice(512, COLS))
    loads = []
    for m, part in enumerate(parts):
        for n in range(4):
            target = wt.at[pl.ds(512 * n, 512), part]
            sem = sems.at[copies.used + 4 * m + n]
            one = pltpu.make_async_copy(mine.at[n, :, part], target, sem)
            two = pltpu.make_async_copy(other.at[n, :, part], target, sem)
            pl.when(half == core)(one.start)
            pl.when(half != core)(two.start)
            loads.append(one)
    copies.wait()
    for m, part in enumerate(parts):
        for one in loads[4 * m : 4 * m + 4]:
            one.wait()

        def tile(n, carry):
            rows = pl.ds(pl.multiple_of(n * 128, 128), 128)
            out[rows, part] = jnp.dot(
                at[rows, :], wt[:, part], preferred_element_type=jnp.float32
            ).astype(out.dtype)
            return carry

        lax.fori_loop(0, HALF // 128, tile, 0)


def project(far, ordered, dtype, pieces, weights):
    return pl.pallas_call(
        functools.partial(project_kernel, far, ordered),
        out_shape=jax.ShapeDtypeStruct((HALF, COLS), dtype),
        in_specs=[ANY] * 7,
        out_specs=VMEM,
        scratch_shapes=[
            pltpu.VMEM((HALF, 2048), jnp.bfloat16),
            pltpu.VMEM((2048, COLS), jnp.bfloat16),
            pltpu.SemaphoreType.DMA((24,)),
        ],
        cost_estimate=pl.CostEstimate(
            flops=2 * HALF * 2048 * COLS, bytes_accessed=5 << 20, transcendentals=0
        ),
        name=f"project{ordered}_" + ("far" if far else "near"),
    )(*pieces, *weights)


def merge(stats, count):
    mean = sum(s[0] for s in stats) / len(stats)
    square = sum(s[1] + count * jnp.square(s[0] - mean) for s in stats)
    return jnp.stack([mean, square])


def shards(
    queries, new_keys, new_values, pool_keys, pool_values, cache_len, cached_table, free_blocks,
    residual_in, out_weight, out_bias, ln_gain, ln_bias,
):
    after = lambda value, *others: lax.optimization_barrier((value, *others))[0]
    group = ("ylo", "core")
    fq, c0, c1, cy = prep(free_blocks, queries, pool_keys, pool_values)

    fq = lax.all_to_all(fq, group, 0, 0)
    cy = move(cy, ("ylo",))
    g0 = jnp.stack([c0, move(c1, ("core",))])
    y0, z0 = move(g0, ("yhi", "ylo")), move(g0, ("zlo",))
    part, keys_out, values_out, f0, f1, fy, early, mid, late = side(
        after(jnp.zeros((1,), jnp.int32), cy), free_blocks, cached_table, cache_len,
        new_keys, new_values, pool_keys, pool_values, out_weight,
    )

    g1 = after(jnp.stack([cy[0], move(cy[1], ("core",))]), y0, z0)
    y1, z1 = move(g1, ("yhi", "ylo")), move(g1, ("zlo",))
    d0 = move(after(y0, g1), ("zlo",))
    fy = move(after(fy, g1), ("ylo",))
    f1 = move(after(f1, g1), ("core",))
    f3 = move(fy[1], ("core",))

    mine = lax.all_to_all(after(part, g1, fq), "x", 0, 0)

    acc, row = attend_early(early, fq, (g0, g1, y0, z0))
    d1 = move(after(z1, acc), ("yhi", "ylo"))
    acc, row = attend_fresh(mid, fq, (f0, f1, fy, f3), (y1, z1), acc, row)
    *mixed0, mixed1 = attend_late(late, fq, (d0, d1), acc, row)

    sums = []
    for ordered, o in enumerate((mixed0, mixed1)):
        if ordered:
            a0 = lax.all_to_all(o, group, 0, 0)
        else:
            a0 = jnp.stack([o[0]] + [move(o[r], RELATION[r]) for r in (1, 2, 3)])
            other = move(after(mine, a0), ("core",))
        ap, am = move(a0, (), 1), move(a0, (), 3)
        pieces = (a0, ap, am, move(ap[:2], (), 1), move(am[2:], (), 3))
        sent = move(project(1, ordered, jnp.bfloat16, pieces, (mine, other)), ("zhi",))
        near = project(0, ordered, jnp.float32, pieces, (mine, other))
        sums.append(near + sent.astype(jnp.float32))
    stream = (
        residual_in.astype(jnp.float32) + jnp.concatenate(sums, axis=0) + out_bias[None, :]
    )
    mean = jnp.sum(stream, axis=1) / COLS
    square = jnp.sum(jnp.square(stream - mean[:, None]), axis=1)
    stats = jnp.stack([mean, square])
    stats = merge([stats] + [move(stats, (), k) for k in (1, 2, 3)], COLS)
    stats = merge([stats, move(stats, ("zhi",))], 4 * COLS)
    mean, variance = stats[0], stats[1] / D
    normed = (
        (stream - mean[:, None]) * lax.rsqrt(variance[:, None] + 1e-05) * ln_gain[None, :]
        + ln_bias[None, :]
    ).astype(jnp.bfloat16)
    return (stream.astype(jnp.bfloat16), normed, keys_out, values_out)


def solution(mesh):
    fine = Mesh(mesh.devices.reshape(tuple(SIZES.values())), tuple(SIZES))
    both = P(SEQ, HEAD)
    head = P(HEAD)
    in_specs = (both,) * 5 + (P(), P(), P()) + (both, P(HEAD, None), head, head, head)
    return jax.shard_map(
        shards, mesh=fine, in_specs=in_specs, out_specs=(both,) * 4, check_vma=False
    )
```

profile of v0, /device:TPU:0, one launch (start us, length us, event | category | flops | bytes accessed | tf_op | source)
XLA Modules:
  0.0 151.1 jit_solution(9889909007752340363)
XLA Ops:
  0.6 3.4 %prep.1 = (bf16[4,512,128]{2,1,0:T(8,128)(2,1)}, bf16[2,512,128]{2,1,0:T(8,128)(2,1)}, bf16[2,512,128]{2,1,0:T(8,128)(2,1)}, bf16[2,2,512,128]{3,2,1,0:T(8,128)(2,1)}) custom-call(s32[4,16]{1,0:T(4,128)} %free.3, bf16[512,512]{1,0:T(8,128)(2,1)} %q.1, bf16[1024,512]{1,0:T(8,128)(2,1)} %pk.3, bf16[1024,512]{1,0:T(8,128)(2,1)} %pv.3), custom_call_target="tpu_custom_call" | custom-call | bytes 4194304 | tf_op jit(solution)/shard_map/prep/pallas_call | solution.py:113
  4.0 1.7 %collective-permute-start = (bf16[2,2,512,128]{3,2,1,0:T(8,128)(2,1)}, bf16[2,2,512,128]{3,2,1,0:T(8,128)(2,1)S(1)}, u32[]{:S(2)}, u32[]{:S(2)}) collective-permute-start(bf16[2,2,512,128]{3,2,1,0:T(8,128)(2,1)} %get-tuple-element.34), channel_id=1, source_target_pairs={{0,16},{16,0},{1,17},{17,1},{2,18},{18,2},{3,19},{19,3},{4,20},{20... | collective-permute-start | bytes 1572872 | tf_op jit(solution)/shard_map/ppermute | solution.py:37
  5.8 3.5 %all-to-all-start = ((bf16[4,512,128]{2,1,0:T(8,128)(2,1)}), bf16[4,512,128]{2,1,0:T(8,128)(2,1)S(1)}, u32[]{:S(2)}, u32[]{:S(2)}) async-start(bf16[4,512,128]{2,1,0:T(8,128)(2,1)} %get-tuple-element.37), calls=%async_computation | async-start | bytes 1048576 | tf_op jit(solution)/shard_map/all_to_all | solution.py:458
  9.2 1.0 pad_maximum_fusion.g0
  10.3 3.5 %collective-permute-start.2 = (bf16[2,2,512,128]{3,2,1,0:T(8,128)(2,1)S(1)}, bf16[2,2,512,128]{3,2,1,0:T(8,128)(2,1)S(1)}, u32[]{:S(2)}, u32[]{:S(2)}) collective-permute-start(bf16[2,2,512,128]{3,2,1,0:T(8,128)(2,1)S(1)} %pad_maximum_fusion.g0), channel_id=1, source_target_pairs={{0,48},{16,32},{32,16},{48,0},{1,49},{17,33},{33,17},{49,1},{2,50}... | collective-permute-start | bytes 1572872 | tf_op jit(solution)/shard_map/ppermute | solution.py:37
  13.8 1.9 %collective-permute-start.4 = (bf16[2,2,512,128]{3,2,1,0:T(8,128)(2,1)S(1)}, bf16[2,2,512,128]{3,2,1,0:T(8,128)(2,1)}, u32[]{:S(2)}, u32[]{:S(2)}) collective-permute-start(bf16[2,2,512,128]{3,2,1,0:T(8,128)(2,1)S(1)} %pad_maximum_fusion.g0), channel_id=1, source_target_pairs={{0,64},{64,0},{1,65},{65,1},{2,66},{66,2},{3,67},{67,3},{4,68},{68... | collective-permute-start | bytes 1572872 | tf_op jit(solution)/shard_map/ppermute | solution.py:37
  15.7 3.5 %collective-permute-done = bf16[2,2,512,128]{3,2,1,0:T(8,128)(2,1)S(1)} collective-permute-done((bf16[2,2,512,128]{3,2,1,0:T(8,128)(2,1)}, bf16[2,2,512,128]{3,2,1,0:T(8,128)(2,1)S(1)}, u32[]{:S(2)}, u32[]{:S(2)}) %collective-permute-start) | collective-permute-done | bytes 524320 | tf_op jit(solution)/shard_map/ppermute | solution.py:37
  19.2 0.1 collective-permute-start.3
  19.3 7.1 %side.1 = (bf16[4,512,896]{2,1,0:T(8,128)(2,1)}, bf16[1024,512]{1,0:T(8,128)(2,1)}, bf16[1024,512]{1,0:T(8,128)(2,1)}, bf16[2,512,128]{2,1,0:T(8,128)(2,1)}, bf1...) custom-call(s32[1]{0:T(128)} %constant.4.clone.1.gate, ...), custom_call_target="tpu_custom_call" | custom-call | bytes 14680064 | tf_op jit(solution)/shard_map/side/pallas_call | solution.py:186
  26.4 0.1 pad_maximum_fusion.1.g1
  26.5 1.2 collective-permute-done.4.z0
  27.8 0.8 copy-done.13
  28.5 4.8 %all-to-all-start.1 = ((bf16[4,512,896]{2,1,0:T(8,128)(2,1)}), bf16[4,512,896]{2,1,0:T(8,128)(2,1)}, u32[]{:S(2)}, u32[]{:S(2)}) async-start(bf16[4,512,896]{2,1,0:T(8,128)(2,1)} %get-tuple-element.59), calls=%async_computation.1 | async-start | bytes 7340032 | tf_op jit(solution)/shard_map/all_to_all | solution.py:474
  33.3 1.8 %collective-permute-start.6 = (bf16[2,2,512,128]{3,2,1,0:T(8,128)(2,1)S(1)}, bf16[2,2,512,128]{3,2,1,0:T(8,128)(2,1)S(1)}, u32[]{:S(2)}, u32[]{:S(2)}) collective-permute-start(bf16[2,2,512,128]{3,2,1,0:T(8,128)(2,1)S(1)} %pad_maximum_fusion.1.g1), channel_id=1, source_target_pairs={{0,64},{64,0},{1,65},{65,1},{2,66},{66,2},{3,67},{67,3},{4,68},{68... | collective-permute-start | bytes 1572872 | tf_op jit(solution)/shard_map/ppermute | solution.py:37
  35.2 0.7 collective-permute-start.9
  35.9 2.2 %collective-permute-start.11 = (bf16[2,2,512,128]{3,2,1,0:T(8,128)(2,1)S(1)}, bf16[2,2,512,128]{3,2,1,0:T(8,128)(2,1)}, u32[]{:S(2)}, u32[]{:S(2)}) collective-permute-start(bf16[2,2,512,128]{3,2,1,0:T(8,128)(2,1)S(1)} %pad_maximum_fusion.1.g1), channel_id=1, source_target_pairs={{0,48},{16,32},{32,16},{48,0},{1,49},{17,33},{33,17},{49,1},{2,50}... | collective-permute-start | bytes 1572872 | tf_op jit(solution)/shard_map/ppermute | solution.py:37
  38.1 0.2 collective-permute-start.5
  38.3 10.4 %attend_early.1 = (f32[128,2048]{1,0:T(8,128)}, f32[8,2048]{1,0:T(8,128)}) custom-call(s32[40]{0:T(128)} %get-tuple-element.42.blocks, bf16[4,512,128]{2,1,0:T(8,128)(2,1)} %copy-done.13, bf16[2,2,512,128]{3,2,1,0:T(8,128)(2,1)} %copy-done.14, bf16[2,2,512,128]{3,2,1,0:T(8,128)(2,1)} %copy-done.15, bf16[2,2,512,128]{3,2,1,0:T(8,128)(2,1)} %copy-done.20, ...), custom_call_target="tpu_custom_call" | custom-call | flops 2048000000 | bytes 4194304 | tf_op jit(solution)/shard_map/attend_early/pallas_call | solution.py:281
  48.7 1.5 %collective-permute-start.7 = (bf16[2,2,512,128]{3,2,1,0:T(8,128)(2,1)S(1)}, bf16[2,2,512,128]{3,2,1,0:T(8,128)(2,1)}, u32[]{:S(2)}, u32[]{:S(2)}) collective-permute-start(bf16[2,2,512,128]{3,2,1,0:T(8,128)(2,1)S(1)} %collective-permute-done.6.z1), channel_id=1, source_target_pairs={{0,48},{16,32},{32,16},{48,0},{1,49},{17,33},{33,17},{49,1},{2,50}... | collective-permute-start | bytes 1572872 | tf_op jit(solution)/shard_map/ppermute | solution.py:37
  50.2 0.3 collective-permute-start.10
  50.5 0.4 collective-permute-done.11.y1
  50.9 1.1 collective-permute-done.10.f3
  52.0 0.7 copy-done.25
  52.7 13.8 %attend_fresh.1 = (f32[128,2048]{1,0:T(8,128)}, f32[8,2048]{1,0:T(8,128)}) custom-call(s32[40]{0:T(128)} %get-tuple-element.45.blocks, bf16[4,512,128]{2,1,0:T(8,128)(2,1)} %copy-done.13, bf16[2,512,128]{2,1,0:T(8,128)(2,1)} %get-tuple-element.46.f0, bf16[2,512,128]{2,1,0:T(8,128)(2,1)} %copy-done.24, bf16[2,2,512,128]{3,2,1,0:T(8,128)(2,1)} %copy-done.16, ...), custom_call_target="tpu_custom_call" | custom-call | flops 1331200000 | bytes 4194304 | tf_op jit(solution)/shard_map/attend_fresh/pallas_call | solution.py:329
  66.6 9.8 %attend_late.1 = (bf16[256,128]{1,0:T(8,128)(2,1)}, bf16[256,128]{1,0:T(8,128)(2,1)}, bf16[256,128]{1,0:T(8,128)(2,1)}, bf16[256,128]{1,0:T(8,128)(2,1)}, bf16[4,256,128]{2,1,0:T(8,128)(2,1)}) custom-call(s32[40]{0:T(128)} %get-tuple-element.36.blocks, bf16[4,512,128]{2,1,0:T(8,128)(2,1)} %copy-done.13, bf16[2,2,512,128]{3,2,1,0:T(8,128)(2,1)} %collective-permute-done.5.d0, ...), custom_call_target="tpu_custom_call" | custom-call | flops 1024000000 | bytes 4194304 | tf_op jit(solution)/shard_map/attend_late/pallas_call | solution.py:370
  76.4 0.4 collective-permute-start.12
  76.8 2.2 %collective-permute-start.13 = (bf16[256,128]{1,0:T(8,128)(2,1)}, bf16[256,128]{1,0:T(8,128)(2,1)S(1)}, u32[]{:S(2)}, u32[]{:S(2)}) collective-permute-start(bf16[256,128]{1,0:T(8,128)(2,1)} %get-tuple-element.56), channel_id=1, source_target_pairs={{0,16},{16,0},{1,17},{17,1},{2,18},{18,2},{3,19},{19,3},{4,20},{20... | collective-permute-start | bytes 196616 | tf_op jit(solution)/shard_map/ppermute | solution.py:37
  79.0 2.7 %collective-permute-done.13 = bf16[256,128]{1,0:T(8,128)(2,1)S(1)} collective-permute-done((bf16[256,128]{1,0:T(8,128)(2,1)}, bf16[256,128]{1,0:T(8,128)(2,1)S(1)}, u32[]{:S(2)}, u32[]{:S(2)}) %collective-permute-start.13) | collective-permute-done | bytes 65568 | tf_op jit(solution)/shard_map/ppermute | solution.py:37
  81.7 1.8 %collective-permute-done.14 = bf16[256,128]{1,0:T(8,128)(2,1)S(1)} collective-permute-done((bf16[256,128]{1,0:T(8,128)(2,1)}, bf16[256,128]{1,0:T(8,128)(2,1)S(1)}, u32[]{:S(2)}, u32[]{:S(2)}) %collective-permute-start.14) | collective-permute-done | bytes 65568 | tf_op jit(solution)/shard_map/ppermute | solution.py:37
  83.5 0.9 pad_maximum_fusion.2.a0
  84.4 0.2 collective-permute-start.19
  84.6 2.0 %collective-permute-start.15 = (bf16[4,256,128]{2,1,0:T(8,128)(2,1)S(1)}, bf16[4,256,128]{2,1,0:T(8,128)(2,1)S(1)}, u32[]{:S(2)}, u32[]{:S(2)}) collective-permute-start(bf16[4,256,128]{2,1,0:T(8,128)(2,1)S(1)} %pad_maximum_fusion.2.a0), channel_id=1, source_target_pairs={{0,1},{1,2},{2,3},{3,0},{4,5},{5,6},{6,7},{7,4},{8,9},{9,10},{10,1... | collective-permute-start | bytes 786440 | tf_op jit(solution)/shard_map/ppermute | solution.py:37
  86.6 1.3 collective-permute-start.16
  87.9 3.4 %all-to-all-start.2 = ((bf16[4,256,128]{2,1,0:T(8,128)(2,1)}), bf16[4,256,128]{2,1,0:T(8,128)(2,1)S(1)}, u32[]{:S(2)}, u32[]{:S(2)}) async-start(bf16[4,256,128]{2,1,0:T(8,128)(2,1)} %get-tuple-element.61), calls=%async_computation.2 | async-start | bytes 524288 | tf_op jit(solution)/shard_map/all_to_all | solution.py:484
  91.3 3.3 %collective-permute-done.15.ap = bf16[4,256,128]{2,1,0:T(8,128)(2,1)S(1)} collective-permute-done((bf16[4,256,128]{2,1,0:T(8,128)(2,1)S(1)}, bf16[4,256,128]{2,1,0:T(8,128)(2,1)S(1)}, u32[]{:S(2)}, u32[]{:S(2)}) %collective-permute-start.15) | collective-permute-done | bytes 262176 | tf_op jit(solution)/shard_map/ppermute | solution.py:37
  94.6 0.6 collective-permute-start.17
  95.2 2.7 %collective-permute-start.18 = (bf16[2,256,128]{2,1,0:T(8,128)(2,1)S(1)}, bf16[2,256,128]{2,1,0:T(8,128)(2,1)S(1)}, u32[]{:S(2)}, u32[]{:S(2)}) collective-permute-start(bf16[2,256,128]{2,1,0:T(8,128)(2,1)S(1)} %slice.68), channel_id=1, source_target_pairs={{0,3},{1,0},{2,1},{3,2},{4,7},{5,4},{6,5},{7,6},{8,11},{9,8},{10,9... | collective-permute-start | bytes 393224 | tf_op jit(solution)/shard_map/ppermute | solution.py:37
  98.0 3.2 %collective-permute-start.22 = (bf16[4,256,128]{2,1,0:T(8,128)(2,1)S(1)}, bf16[4,256,128]{2,1,0:T(8,128)(2,1)S(1)}, u32[]{:S(2)}, u32[]{:S(2)}) collective-permute-start(bf16[4,256,128]{2,1,0:T(8,128)(2,1)S(1)} %all-to-all-done.2.a0), channel_id=1, source_target_pairs={{0,3},{1,0},{2,1},{3,2},{4,7},{5,4},{6,5},{7,6},{8,11},{9,8},{10,9... | collective-permute-start | bytes 786440 | tf_op jit(solution)/shard_map/ppermute | solution.py:37
  101.3 0.6 copy-done.9
  101.9 4.8 %project0_far.1 = bf16[256,896]{1,0:T(8,128)(2,1)} custom-call(bf16[4,256,128]{2,1,0:T(8,128)(2,1)} %copy-done.3, bf16[4,256,128]{2,1,0:T(8,128)(2,1)} %copy-done.5, bf16[4,256,128]{2,1,0:T(8,128)(2,1)} %copy-done.6, bf16[2,256,128]{2,1,0:T(8,128)(2,1)} %copy-done.9, bf16[2,256,128]{2,1,0:T(8,128)(2,1)} %copy-done.10, ...), custom_call_target="tpu_custom_call" | custom-call | flops 939524096 | bytes 5242880 | tf_op jit(solution)/shard_map/project0_far/pallas_call | solution.py:427
  106.7 3.7 %collective-permute-start.20 = (bf16[256,896]{1,0:T(8,128)(2,1)}, bf16[256,896]{1,0:T(8,128)(2,1)S(1)}, u32[]{:S(2)}, u32[]{:S(2)}) collective-permute-start(bf16[256,896]{1,0:T(8,128)(2,1)} %project0_far.1), channel_id=1, source_target_pairs={{0,4},{4,0},{1,5},{5,1},{2,6},{6,2},{3,7},{7,3},{8,12},{12,8},{9,1... | collective-permute-start | bytes 1376264 | tf_op jit(solution)/shard_map/ppermute | solution.py:37
  110.4 0.8 collective-permute-start.23
  111.2 2.6 %collective-permute-start.24 = (bf16[2,256,128]{2,1,0:T(8,128)(2,1)S(1)}, bf16[2,256,128]{2,1,0:T(8,128)(2,1)S(1)}, u32[]{:S(2)}, u32[]{:S(2)}) collective-permute-start(bf16[2,256,128]{2,1,0:T(8,128)(2,1)S(1)} %slice.70), channel_id=1, source_target_pairs={{0,3},{1,0},{2,1},{3,2},{4,7},{5,4},{6,5},{7,6},{8,11},{9,8},{10,9... | collective-permute-start | bytes 393224 | tf_op jit(solution)/shard_map/ppermute | solution.py:37
  113.8 2.9 %collective-permute-done.23.a2a = bf16[2,256,128]{2,1,0:T(8,128)(2,1)S(1)} collective-permute-done((bf16[2,256,128]{2,1,0:T(8,128)(2,1)S(1)}, bf16[2,256,128]{2,1,0:T(8,128)(2,1)S(1)}, u32[]{:S(2)}, u32[]{:S(2)}) %collective-permute-start.23) | collective-permute-done | bytes 131104 | tf_op jit(solution)/shard_map/ppermute | solution.py:37
  116.7 0.6 copy-done.11
  117.3 0.6 copy-done.12
  118.0 4.8 %project1_far.1 = bf16[256,896]{1,0:T(8,128)(2,1)} custom-call(bf16[4,256,128]{2,1,0:T(8,128)(2,1)} %copy-done.4, bf16[4,256,128]{2,1,0:T(8,128)(2,1)} %copy-done.7, bf16[4,256,128]{2,1,0:T(8,128)(2,1)} %copy-done.8, bf16[2,256,128]{2,1,0:T(8,128)(2,1)} %copy-done.11, bf16[2,256,128]{2,1,0:T(8,128)(2,1)} %copy-done.12, ...), custom_call_target="tpu_custom_call" | custom-call | flops 939524096 | bytes 5242880 | tf_op jit(solution)/shard_map/project1_far/pallas_call | solution.py:427
  122.8 0.1 collective-permute-start.25
  122.9 4.9 %project0_near.1 = f32[256,896]{1,0:T(8,128)} custom-call(bf16[4,256,128]{2,1,0:T(8,128)(2,1)} %copy-done.3, bf16[4,256,128]{2,1,0:T(8,128)(2,1)} %copy-done.5, bf16[4,256,128]{2,1,0:T(8,128)(2,1)} %copy-done.6, bf16[2,256,128]{2,1,0:T(8,128)(2,1)} %copy-done.9, bf16[2,256,128]{2,1,0:T(8,128)(2,1)} %copy-done.10, bf16[4,512,896]{2,1,0:T(8,128)(2,1)} %all-to-all-done.1.mine, ...), custom_call_target="tpu_custom_call" | custom-call | flops 939524096 | bytes 5242880 | tf_op jit(solution)/shard_map/project0_near/pallas_call | solution.py:427
  127.8 4.9 %project1_near.1 = f32[256,896]{1,0:T(8,128)} custom-call(bf16[4,256,128]{2,1,0:T(8,128)(2,1)} %copy-done.4, bf16[4,256,128]{2,1,0:T(8,128)(2,1)} %copy-done.7, bf16[4,256,128]{2,1,0:T(8,128)(2,1)} %copy-done.8, bf16[2,256,128]{2,1,0:T(8,128)(2,1)} %copy-done.11, bf16[2,256,128]{2,1,0:T(8,128)(2,1)} %copy-done.12, bf16[4,512,896]{2,1,0:T(8,128)(2,1)} %all-to-all-done.1.mine, ...), custom_call_target="tpu_custom_call" | custom-call | flops 939524096 | bytes 5242880 | tf_op jit(solution)/shard_map/project1_near/pallas_call | solution.py:427
  132.8 0.1 convert_add_fusion.1
  132.9 1.8 %collective-permute-done.25 = bf16[256,896]{1,0:T(8,128)(2,1)} collective-permute-done((bf16[256,896]{1,0:T(8,128)(2,1)}, bf16[256,896]{1,0:T(8,128)(2,1)}, u32[]{:S(2)}, u32[]{:S(2)}) %collective-permute-start.25) | collective-permute-done | bytes 458784 | tf_op jit(solution)/shard_map/ppermute | solution.py:37
  134.6 1.1 convert_add_fusion
  135.7 0.3 fusion.1
  136.1 0.5 multiply_reduce_fusion
  136.6 0.2 collective-permute-start.26
  136.8 3.7 %collective-permute-start.27 = (f32[2,512]{1,0:T(2,128)S(1)}, f32[2,512]{1,0:T(2,128)S(1)}, u32[]{:S(2)}, u32[]{:S(2)}) collective-permute-start(f32[2,512]{1,0:T(2,128)S(1)} %pad_maximum_fusion.3), channel_id=1, source_target_pairs={{0,2},{1,3},{2,0},{3,1},{4,6},{5,7},{6,4},{7,5},{8,10},{9,11},{10,... | collective-permute-start | bytes 12296 | tf_op jit(solution)/shard_map/ppermute | solution.py:37
  140.5 0.8 collective-permute-start.28
  141.3 0.1 collective-permute-done.26
  141.4 0.7 collective-permute-done.27
  142.1 2.0 %collective-permute-done.28 = f32[2,512]{1,0:T(2,128)S(1)} collective-permute-done((f32[2,512]{1,0:T(2,128)S(1)}, f32[2,512]{1,0:T(2,128)S(1)}, u32[]{:S(2)}, u32[]{:S(2)}) %collective-permute-start.28) | collective-permute-done | bytes 4128 | tf_op jit(solution)/shard_map/ppermute | solution.py:37
  144.2 3.1 %collective-permute-start.29 = (f32[2,512]{1,0:T(2,128)S(1)}, f32[2,512]{1,0:T(2,128)S(1)}, u32[]{:S(2)}, u32[]{:S(2)}) collective-permute-start(f32[2,512]{1,0:T(2,128)S(1)} %pad_maximum_fusion.4), channel_id=1, source_target_pairs={{0,4},{4,0},{1,5},{5,1},{2,6},{6,2},{3,7},{7,3},{8,12},{12,8},{9,1... | collective-permute-start | bytes 12296 | tf_op jit(solution)/shard_map/ppermute | solution.py:37
  147.3 2.1 %collective-permute-done.29 = f32[2,512]{1,0:T(2,128)S(1)} collective-permute-done((f32[2,512]{1,0:T(2,128)S(1)}, f32[2,512]{1,0:T(2,128)S(1)}, u32[]{:S(2)}, u32[]{:S(2)}) %collective-permute-start.29) | collective-permute-done | bytes 4128 | tf_op jit(solution)/shard_map/ppermute | solution.py:37
  149.4 1.8 %add_convert_fusion = (bf16[512,896]{1,0:T(8,128)(2,1)}, bf16[512,896]{1,0:T(8,128)(2,1)}) fusion(f32[896]{0:T(1024)S(1)} %copy-done.18, f32[896]{0:T(1024)S(1)} %copy-done.19, f32[512]{0:T(512)S(1)} %get-tuple-element.71, f32[512]{0:T(512)S(1)} %get-tuple-element.70, f32[896]{0:T(1024)S(1)} %copy-done.17, f32[256,896]{1,0:T(8,128)S(1)} %convert_add_fusion, ...), kind=kLoop, calls=%fused_computation.2 | loop fusion | flops 4587520 | bytes 4602368 | tf_op jit(solution)/shard_map/convert_element_type | solution.py:505
  (83 shorter events, 0.4 us)
Async XLA Ops:
  4.0 15.1 %collective-permute-start = (bf16[2,2,512,128]{3,2,1,0:T(8,128)(2,1)}, bf16[2,2,512,128]{3,2,1,0:T(8,128)(2,1)S(1)}, u32[]{:S(2)}, u32[]{:S(2)}) collective-permute-start(bf16[2,2,512,128]{3,2,1,0:T(8,128)(2,1)} %get-tuple-element.34), channel_id=1, source_target_pairs={{0,16},{16,0},{1,17},{17,1},{2,18},{18,2},{3,19},{19,3},{4,20},{20... | collective-permute-start | bytes 1572872 | tf_op jit(solution)/shard_map/ppermute | solution.py:37
  5.8 3.5 %collective-permute-start.1 = (bf16[2,512,128]{2,1,0:T(8,128)(2,1)}, bf16[2,512,128]{2,1,0:T(8,128)(2,1)S(1)}, u32[]{:S(2)}, u32[]{:S(2)}) collective-permute-start(bf16[2,512,128]{2,1,0:T(8,128)(2,1)} %get-tuple-element.39), channel_id=1, source_target_pairs={{0,8},{8,0},{1,9},{9,1},{2,10},{10,2},{3,11},{11,3},{4,12},{12,4},... | collective-permute-start | bytes 786440 | tf_op jit(solution)/shard_map/ppermute | solution.py:37
  5.8 22.0 %all-to-all-start = ((bf16[4,512,128]{2,1,0:T(8,128)(2,1)}), bf16[4,512,128]{2,1,0:T(8,128)(2,1)S(1)}, u32[]{:S(2)}, u32[]{:S(2)}) async-start(bf16[4,512,128]{2,1,0:T(8,128)(2,1)} %get-tuple-element.37), calls=%async_computation | async-start | bytes 1048576 | tf_op jit(solution)/shard_map/all_to_all | solution.py:458
  10.3 16.1 %copy-start.14 = (bf16[2,2,512,128]{3,2,1,0:T(8,128)(2,1)}, bf16[2,2,512,128]{3,2,1,0:T(8,128)(2,1)S(1)}, u32[]{:S(2)}) copy-start(bf16[2,2,512,128]{3,2,1,0:T(8,128)(2,1)S(1)} %pad_maximum_fusion.g0) | copy-start | bytes 1572868
  10.3 16.2 %collective-permute-start.2 = (bf16[2,2,512,128]{3,2,1,0:T(8,128)(2,1)S(1)}, bf16[2,2,512,128]{3,2,1,0:T(8,128)(2,1)S(1)}, u32[]{:S(2)}, u32[]{:S(2)}) collective-permute-start(bf16[2,2,512,128]{3,2,1,0:T(8,128)(2,1)S(1)} %pad_maximum_fusion.g0), channel_id=1, source_target_pairs={{0,48},{16,32},{32,16},{48,0},{1,49},{17,33},{33,17},{49,1},{2,50}... | collective-permute-start | bytes 1572872 | tf_op jit(solution)/shard_map/ppermute | solution.py:37
  13.8 14.0 %collective-permute-start.4 = (bf16[2,2,512,128]{3,2,1,0:T(8,128)(2,1)S(1)}, bf16[2,2,512,128]{3,2,1,0:T(8,128)(2,1)}, u32[]{:S(2)}, u32[]{:S(2)}) collective-permute-start(bf16[2,2,512,128]{3,2,1,0:T(8,128)(2,1)S(1)} %pad_maximum_fusion.g0), channel_id=1, source_target_pairs={{0,64},{64,0},{1,65},{65,1},{2,66},{66,2},{3,67},{67,3},{4,68},{68... | collective-permute-start | bytes 1572872 | tf_op jit(solution)/shard_map/ppermute | solution.py:37
  19.2 7.2 %collective-permute-start.3 = (bf16[2,512,128]{2,1,0:T(8,128)(2,1)S(1)}, bf16[2,512,128]{2,1,0:T(8,128)(2,1)S(1)}, u32[]{:S(2)}, u32[]{:S(2)}) collective-permute-start(bf16[2,512,128]{2,1,0:T(8,128)(2,1)S(1)} %get-tuple-element.69), channel_id=1, source_target_pairs={{0,8},{8,0},{1,9},{9,1},{2,10},{10,2},{3,11},{11,3},{4,12},{12,4},... | collective-permute-start | bytes 786440 | tf_op jit(solution)/shard_map/ppermute | solution.py:37
  26.5 9.4 %copy-start.15 = (bf16[2,2,512,128]{3,2,1,0:T(8,128)(2,1)}, bf16[2,2,512,128]{3,2,1,0:T(8,128)(2,1)S(1)}, u32[]{:S(2)}) copy-start(bf16[2,2,512,128]{3,2,1,0:T(8,128)(2,1)S(1)} %pad_maximum_fusion.1.g1) | copy-start | bytes 1572868
  26.5 11.6 %copy-start.20 = (bf16[2,2,512,128]{3,2,1,0:T(8,128)(2,1)}, bf16[2,2,512,128]{3,2,1,0:T(8,128)(2,1)S(1)}, u32[]{:S(2)}) copy-start(bf16[2,2,512,128]{3,2,1,0:T(8,128)(2,1)S(1)} %collective-permute-done.2.y0) | copy-start | bytes 1572868
  27.7 0.8 copy-start.13
  27.7 7.4 %copy-start.21 = (bf16[2,2,512,128]{3,2,1,0:T(8,128)(2,1)S(1)}, bf16[2,2,512,128]{3,2,1,0:T(8,128)(2,1)}, u32[]{:S(2)}) copy-start(bf16[2,2,512,128]{3,2,1,0:T(8,128)(2,1)} %get-tuple-element.50) | copy-start | bytes 1572868
  27.7 10.3 %copy-start.23 = (bf16[2,512,128]{2,1,0:T(8,128)(2,1)S(1)}, bf16[2,512,128]{2,1,0:T(8,128)(2,1)}, u32[]{:S(2)}) copy-start(bf16[2,512,128]{2,1,0:T(8,128)(2,1)} %get-tuple-element.48) | copy-start | bytes 786436
  28.5 55.9 %all-to-all-start.1 = ((bf16[4,512,896]{2,1,0:T(8,128)(2,1)}), bf16[4,512,896]{2,1,0:T(8,128)(2,1)}, u32[]{:S(2)}, u32[]{:S(2)}) async-start(bf16[4,512,896]{2,1,0:T(8,128)(2,1)} %get-tuple-element.59), calls=%async_computation.1 | async-start | bytes 7340032 | tf_op jit(solution)/shard_map/all_to_all | solution.py:474
  33.3 15.3 %collective-permute-start.6 = (bf16[2,2,512,128]{3,2,1,0:T(8,128)(2,1)S(1)}, bf16[2,2,512,128]{3,2,1,0:T(8,128)(2,1)S(1)}, u32[]{:S(2)}, u32[]{:S(2)}) collective-permute-start(bf16[2,2,512,128]{3,2,1,0:T(8,128)(2,1)S(1)} %pad_maximum_fusion.1.g1), channel_id=1, source_target_pairs={{0,64},{64,0},{1,65},{65,1},{2,66},{66,2},{3,67},{67,3},{4,68},{68... | collective-permute-start | bytes 1572872 | tf_op jit(solution)/shard_map/ppermute | solution.py:37
  35.2 15.0 %collective-permute-start.9 = (bf16[2,2,512,128]{3,2,1,0:T(8,128)(2,1)S(1)}, bf16[2,2,512,128]{3,2,1,0:T(8,128)(2,1)S(1)}, u32[]{:S(2)}, u32[]{:S(2)}) collective-permute-start(bf16[2,2,512,128]{3,2,1,0:T(8,128)(2,1)S(1)} %copy-done.21), channel_id=1, source_target_pairs={{0,16},{16,0},{1,17},{17,1},{2,18},{18,2},{3,19},{19,3},{4,20},{20... | collective-permute-start | bytes 1572872 | tf_op jit(solution)/shard_map/ppermute | solution.py:37
  35.9 15.1 %collective-permute-start.11 = (bf16[2,2,512,128]{3,2,1,0:T(8,128)(2,1)S(1)}, bf16[2,2,512,128]{3,2,1,0:T(8,128)(2,1)}, u32[]{:S(2)}, u32[]{:S(2)}) collective-permute-start(bf16[2,2,512,128]{3,2,1,0:T(8,128)(2,1)S(1)} %pad_maximum_fusion.1.g1), channel_id=1, source_target_pairs={{0,48},{16,32},{32,16},{48,0},{1,49},{17,33},{33,17},{49,1},{2,50}... | collective-permute-start | bytes 1572872 | tf_op jit(solution)/shard_map/ppermute | solution.py:37
  38.1 12.4 %collective-permute-start.8 = (bf16[2,512,128]{2,1,0:T(8,128)(2,1)S(1)}, bf16[2,512,128]{2,1,0:T(8,128)(2,1)S(1)}, u32[]{:S(2)}, u32[]{:S(2)}) collective-permute-start(bf16[2,512,128]{2,1,0:T(8,128)(2,1)S(1)} %copy-done.23), channel_id=1, source_target_pairs={{0,8},{8,0},{1,9},{9,1},{2,10},{10,2},{3,11},{11,3},{4,12},{12,4},... | collective-permute-start | bytes 786440 | tf_op jit(solution)/shard_map/ppermute | solution.py:37
  38.1 28.5 %collective-permute-start.5 = (bf16[2,2,512,128]{3,2,1,0:T(8,128)(2,1)S(1)}, bf16[2,2,512,128]{3,2,1,0:T(8,128)(2,1)}, u32[]{:S(2)}, u32[]{:S(2)}) collective-permute-start(bf16[2,2,512,128]{3,2,1,0:T(8,128)(2,1)S(1)} %collective-permute-done.2.y0), channel_id=1, source_target_pairs={{0,64},{64,0},{1,65},{65,1},{2,66},{66,2},{3,67},{67,3},{4,68},{68... | collective-permute-start | bytes 1572872 | tf_op jit(solution)/shard_map/ppermute | solution.py:37
  48.6 3.4 %copy-start.22 = (bf16[2,2,512,128]{3,2,1,0:T(8,128)(2,1)}, bf16[2,2,512,128]{3,2,1,0:T(8,128)(2,1)S(1)}, u32[]{:S(2)}) copy-start(bf16[2,2,512,128]{3,2,1,0:T(8,128)(2,1)S(1)} %collective-permute-done.6.z1) | copy-start | bytes 1572868
  48.7 17.9 %collective-permute-start.7 = (bf16[2,2,512,128]{3,2,1,0:T(8,128)(2,1)S(1)}, bf16[2,2,512,128]{3,2,1,0:T(8,128)(2,1)}, u32[]{:S(2)}, u32[]{:S(2)}) collective-permute-start(bf16[2,2,512,128]{3,2,1,0:T(8,128)(2,1)S(1)} %collective-permute-done.6.z1), channel_id=1, source_target_pairs={{0,48},{16,32},{32,16},{48,0},{1,49},{17,33},{33,17},{49,1},{2,50}... | collective-permute-start | bytes 1572872 | tf_op jit(solution)/shard_map/ppermute | solution.py:37
  50.2 1.8 %copy-start.16 = (bf16[2,2,512,128]{3,2,1,0:T(8,128)(2,1)}, bf16[2,2,512,128]{3,2,1,0:T(8,128)(2,1)S(1)}, u32[]{:S(2)}) copy-start(bf16[2,2,512,128]{3,2,1,0:T(8,128)(2,1)S(1)} %collective-permute-done.9.fy) | copy-start | bytes 1572868
  50.2 1.8 %collective-permute-start.10 = (bf16[2,512,128]{2,1,0:T(8,128)(2,1)S(1)}, bf16[2,512,128]{2,1,0:T(8,128)(2,1)S(1)}, u32[]{:S(2)}, u32[]{:S(2)}) collective-permute-start(bf16[2,512,128]{2,1,0:T(8,128)(2,1)S(1)} %slice_bitcast_fusion), channel_id=1, source_target_pairs={{0,8},{8,0},{1,9},{9,1},{2,10},{10,2},{3,11},{11,3},{4,12},{12,4},... | collective-permute-start | bytes 786440 | tf_op jit(solution)/shard_map/ppermute | solution.py:37
  50.5 1.5 %copy-start.24 = (bf16[2,512,128]{2,1,0:T(8,128)(2,1)}, bf16[2,512,128]{2,1,0:T(8,128)(2,1)S(1)}, u32[]{:S(2)}) copy-start(bf16[2,512,128]{2,1,0:T(8,128)(2,1)S(1)} %collective-permute-done.8.f1) | copy-start | bytes 786436
  52.0 0.7 copy-start.25
  76.4 2.6 %collective-permute-start.12 = (bf16[256,128]{1,0:T(8,128)(2,1)}, bf16[256,128]{1,0:T(8,128)(2,1)S(1)}, u32[]{:S(2)}, u32[]{:S(2)}) collective-permute-start(bf16[256,128]{1,0:T(8,128)(2,1)} %get-tuple-element.55), channel_id=1, source_target_pairs={{0,8},{8,0},{1,9},{9,1},{2,10},{10,2},{3,11},{11,3},{4,12},{12,4},... | collective-permute-start | bytes 196616 | tf_op jit(solution)/shard_map/ppermute | solution.py:37
  76.8 4.9 %collective-permute-start.13 = (bf16[256,128]{1,0:T(8,128)(2,1)}, bf16[256,128]{1,0:T(8,128)(2,1)S(1)}, u32[]{:S(2)}, u32[]{:S(2)}) collective-permute-start(bf16[256,128]{1,0:T(8,128)(2,1)} %get-tuple-element.56), channel_id=1, source_target_pairs={{0,16},{16,0},{1,17},{17,1},{2,18},{18,2},{3,19},{19,3},{4,20},{20... | collective-permute-start | bytes 196616 | tf_op jit(solution)/shard_map/ppermute | solution.py:37
  79.0 4.5 %collective-permute-start.14 = (bf16[256,128]{1,0:T(8,128)(2,1)}, bf16[256,128]{1,0:T(8,128)(2,1)S(1)}, u32[]{:S(2)}, u32[]{:S(2)}) collective-permute-start(bf16[256,128]{1,0:T(8,128)(2,1)} %get-tuple-element.57), channel_id=1, source_target_pairs={{0,24},{8,16},{16,8},{24,0},{1,25},{9,17},{17,9},{25,1},{2,26},{10... | collective-permute-start | bytes 196616 | tf_op jit(solution)/shard_map/ppermute | solution.py:37
  84.4 16.9 %copy-start.3 = (bf16[4,256,128]{2,1,0:T(8,128)(2,1)}, bf16[4,256,128]{2,1,0:T(8,128)(2,1)S(1)}, u32[]{:S(2)}) copy-start(bf16[4,256,128]{2,1,0:T(8,128)(2,1)S(1)} %pad_maximum_fusion.2.a0) | copy-start | bytes 786436
  84.4 16.8 %collective-permute-start.19 = (bf16[4,512,896]{2,1,0:T(8,128)(2,1)}, bf16[4,512,896]{2,1,0:T(8,128)(2,1)}, u32[]{:S(2)}, u32[]{:S(2)}) collective-permute-start(bf16[4,512,896]{2,1,0:T(8,128)(2,1)} %all-to-all-done.1.mine), channel_id=1, source_target_pairs={{0,8},{8,0},{1,9},{9,1},{2,10},{10,2},{3,11},{11,3},{4,12},{12,4},... | collective-permute-start | bytes 11010056 | tf_op jit(solution)/shard_map/ppermute | solution.py:37
  84.6 10.0 %collective-permute-start.15 = (bf16[4,256,128]{2,1,0:T(8,128)(2,1)S(1)}, bf16[4,256,128]{2,1,0:T(8,128)(2,1)S(1)}, u32[]{:S(2)}, u32[]{:S(2)}) collective-permute-start(bf16[4,256,128]{2,1,0:T(8,128)(2,1)S(1)} %pad_maximum_fusion.2.a0), channel_id=1, source_target_pairs={{0,1},{1,2},{2,3},{3,0},{4,5},{5,6},{6,7},{7,4},{8,9},{9,10},{10,1... | collective-permute-start | bytes 786440 | tf_op jit(solution)/shard_map/ppermute | solution.py:37
  86.6 8.7 %collective-permute-start.16 = (bf16[4,256,128]{2,1,0:T(8,128)(2,1)S(1)}, bf16[4,256,128]{2,1,0:T(8,128)(2,1)S(1)}, u32[]{:S(2)}, u32[]{:S(2)}) collective-permute-start(bf16[4,256,128]{2,1,0:T(8,128)(2,1)S(1)} %pad_maximum_fusion.2.a0), channel_id=1, source_target_pairs={{0,3},{1,0},{2,1},{3,2},{4,7},{5,4},{6,5},{7,6},{8,11},{9,8},{10,9... | collective-permute-start | bytes 786440 | tf_op jit(solution)/shard_map/ppermute | solution.py:37
  87.9 10.1 %all-to-all-start.2 = ((bf16[4,256,128]{2,1,0:T(8,128)(2,1)}), bf16[4,256,128]{2,1,0:T(8,128)(2,1)S(1)}, u32[]{:S(2)}, u32[]{:S(2)}) async-start(bf16[4,256,128]{2,1,0:T(8,128)(2,1)} %get-tuple-element.61), calls=%async_computation.2 | async-start | bytes 524288 | tf_op jit(solution)/shard_map/all_to_all | solution.py:484
  94.6 6.7 %copy-start.5 = (bf16[4,256,128]{2,1,0:T(8,128)(2,1)}, bf16[4,256,128]{2,1,0:T(8,128)(2,1)S(1)}, u32[]{:S(2)}) copy-start(bf16[4,256,128]{2,1,0:T(8,128)(2,1)S(1)} %collective-permute-done.15.ap) | copy-start | bytes 786436
  94.6 6.6 %collective-permute-start.17 = (bf16[2,256,128]{2,1,0:T(8,128)(2,1)S(1)}, bf16[2,256,128]{2,1,0:T(8,128)(2,1)S(1)}, u32[]{:S(2)}, u32[]{:S(2)}) collective-permute-start(bf16[2,256,128]{2,1,0:T(8,128)(2,1)S(1)} %slice.67), channel_id=1, source_target_pairs={{0,1},{1,2},{2,3},{3,0},{4,5},{5,6},{6,7},{7,4},{8,9},{9,10},{10,1... | collective-permute-start | bytes 393224 | tf_op jit(solution)/shard_map/ppermute | solution.py:37
  95.2 6.1 %copy-start.6 = (bf16[4,256,128]{2,1,0:T(8,128)(2,1)}, bf16[4,256,128]{2,1,0:T(8,128)(2,1)S(1)}, u32[]{:S(2)}) copy-start(bf16[4,256,128]{2,1,0:T(8,128)(2,1)S(1)} %collective-permute-done.16.am) | copy-start | bytes 786436
  95.2 6.0 %collective-permute-start.18 = (bf16[2,256,128]{2,1,0:T(8,128)(2,1)S(1)}, bf16[2,256,128]{2,1,0:T(8,128)(2,1)S(1)}, u32[]{:S(2)}, u32[]{:S(2)}) collective-permute-start(bf16[2,256,128]{2,1,0:T(8,128)(2,1)S(1)} %slice.68), channel_id=1, source_target_pairs={{0,3},{1,0},{2,1},{3,2},{4,7},{5,4},{6,5},{7,6},{8,11},{9,8},{10,9... | collective-permute-start | bytes 393224 | tf_op jit(solution)/shard_map/ppermute | solution.py:37
  98.0 8.7 %copy-start.4 = (bf16[4,256,128]{2,1,0:T(8,128)(2,1)}, bf16[4,256,128]{2,1,0:T(8,128)(2,1)S(1)}, u32[]{:S(2)}) copy-start(bf16[4,256,128]{2,1,0:T(8,128)(2,1)S(1)} %all-to-all-done.2.a0) | copy-start | bytes 786436
  98.0 12.4 %collective-permute-start.21 = (bf16[4,256,128]{2,1,0:T(8,128)(2,1)S(1)}, bf16[4,256,128]{2,1,0:T(8,128)(2,1)S(1)}, u32[]{:S(2)}, u32[]{:S(2)}) collective-permute-start(bf16[4,256,128]{2,1,0:T(8,128)(2,1)S(1)} %all-to-all-done.2.a0), channel_id=1, source_target_pairs={{0,1},{1,2},{2,3},{3,0},{4,5},{5,6},{6,7},{7,4},{8,9},{9,10},{10,1... | collective-permute-start | bytes 786440 | tf_op jit(solution)/shard_map/ppermute | solution.py:37
  98.0 13.2 %collective-permute-start.22 = (bf16[4,256,128]{2,1,0:T(8,128)(2,1)S(1)}, bf16[4,256,128]{2,1,0:T(8,128)(2,1)S(1)}, u32[]{:S(2)}, u32[]{:S(2)}) collective-permute-start(bf16[4,256,128]{2,1,0:T(8,128)(2,1)S(1)} %all-to-all-done.2.a0), channel_id=1, source_target_pairs={{0,3},{1,0},{2,1},{3,2},{4,7},{5,4},{6,5},{7,6},{8,11},{9,8},{10,9... | collective-permute-start | bytes 786440 | tf_op jit(solution)/shard_map/ppermute | solution.py:37
  101.2 0.7 copy-start.9
  101.2 0.7 copy-start.10
  106.7 26.0 %collective-permute-start.20 = (bf16[256,896]{1,0:T(8,128)(2,1)}, bf16[256,896]{1,0:T(8,128)(2,1)S(1)}, u32[]{:S(2)}, u32[]{:S(2)}) collective-permute-start(bf16[256,896]{1,0:T(8,128)(2,1)} %project0_far.1), channel_id=1, source_target_pairs={{0,4},{4,0},{1,5},{5,1},{2,6},{6,2},{3,7},{7,3},{8,12},{12,8},{9,1... | collective-permute-start | bytes 1376264 | tf_op jit(solution)/shard_map/ppermute | solution.py:37
  110.4 6.3 %copy-start.7 = (bf16[4,256,128]{2,1,0:T(8,128)(2,1)}, bf16[4,256,128]{2,1,0:T(8,128)(2,1)S(1)}, u32[]{:S(2)}) copy-start(bf16[4,256,128]{2,1,0:T(8,128)(2,1)S(1)} %collective-permute-done.21.ap) | copy-start | bytes 786436
  110.4 6.2 %collective-permute-start.23 = (bf16[2,256,128]{2,1,0:T(8,128)(2,1)S(1)}, bf16[2,256,128]{2,1,0:T(8,128)(2,1)S(1)}, u32[]{:S(2)}, u32[]{:S(2)}) collective-permute-start(bf16[2,256,128]{2,1,0:T(8,128)(2,1)S(1)} %slice.69), channel_id=1, source_target_pairs={{0,1},{1,2},{2,3},{3,0},{4,5},{5,6},{6,7},{7,4},{8,9},{9,10},{10,1... | collective-permute-start | bytes 393224 | tf_op jit(solution)/shard_map/ppermute | solution.py:37
  111.2 5.5 %copy-start.8 = (bf16[4,256,128]{2,1,0:T(8,128)(2,1)}, bf16[4,256,128]{2,1,0:T(8,128)(2,1)S(1)}, u32[]{:S(2)}) copy-start(bf16[4,256,128]{2,1,0:T(8,128)(2,1)S(1)} %collective-permute-done.22.am) | copy-start | bytes 786436
  111.2 5.5 %collective-permute-start.24 = (bf16[2,256,128]{2,1,0:T(8,128)(2,1)S(1)}, bf16[2,256,128]{2,1,0:T(8,128)(2,1)S(1)}, u32[]{:S(2)}, u32[]{:S(2)}) collective-permute-start(bf16[2,256,128]{2,1,0:T(8,128)(2,1)S(1)} %slice.70), channel_id=1, source_target_pairs={{0,3},{1,0},{2,1},{3,2},{4,7},{5,4},{6,5},{7,6},{8,11},{9,8},{10,9... | collective-permute-start | bytes 393224 | tf_op jit(solution)/shard_map/ppermute | solution.py:37
  116.7 0.6 copy-start.11
  117.3 0.6 copy-start.12
  122.8 11.9 %collective-permute-start.25 = (bf16[256,896]{1,0:T(8,128)(2,1)}, bf16[256,896]{1,0:T(8,128)(2,1)}, u32[]{:S(2)}, u32[]{:S(2)}) collective-permute-start(bf16[256,896]{1,0:T(8,128)(2,1)} %project1_far.1), channel_id=1, source_target_pairs={{0,4},{4,0},{1,5},{5,1},{2,6},{6,2},{3,7},{7,3},{8,12},{12,8},{9,1... | collective-permute-start | bytes 1376264 | tf_op jit(solution)/shard_map/ppermute | solution.py:37
  127.8 5.0 %copy-start.2 = (f32[256,896]{1,0:T(8,128)S(1)}, f32[256,896]{1,0:T(8,128)}, u32[]{:S(2)}) copy-start(f32[256,896]{1,0:T(8,128)} %project0_near.1) | copy-start | bytes 2752516
  132.7 1.9 %copy-start.1 = (f32[256,896]{1,0:T(8,128)S(1)}, f32[256,896]{1,0:T(8,128)}, u32[]{:S(2)}) copy-start(f32[256,896]{1,0:T(8,128)} %project1_near.1) | copy-start | bytes 2752516
  132.7 3.0 %copy-start = (bf16[512,896]{1,0:T(8,128)(2,1)S(1)}, bf16[512,896]{1,0:T(8,128)(2,1)}, u32[]{:S(2)}) copy-start(bf16[512,896]{1,0:T(8,128)(2,1)} %param.21) | copy-start | bytes 2752516
  132.7 3.0 %copy-start.17 = (f32[896]{0:T(1024)S(1)}, f32[896]{0:T(1024)}, u32[]{:S(2)}) copy-start(f32[896]{0:T(1024)} %param.23) | copy-start | bytes 10756
  136.1 13.3 %copy-start.18 = (f32[896]{0:T(1024)S(1)}, f32[896]{0:T(1024)}, u32[]{:S(2)}) copy-start(f32[896]{0:T(1024)} %param.25) | copy-start | bytes 10756
  136.1 13.3 %copy-start.19 = (f32[896]{0:T(1024)S(1)}, f32[896]{0:T(1024)}, u32[]{:S(2)}) copy-start(f32[896]{0:T(1024)} %param.24) | copy-start | bytes 10756
  136.6 4.9 %collective-permute-start.26 = (f32[2,512]{1,0:T(2,128)S(1)}, f32[2,512]{1,0:T(2,128)S(1)}, u32[]{:S(2)}, u32[]{:S(2)}) collective-permute-start(f32[2,512]{1,0:T(2,128)S(1)} %pad_maximum_fusion.3), channel_id=1, source_target_pairs={{0,1},{1,2},{2,3},{3,0},{4,5},{5,6},{6,7},{7,4},{8,9},{9,10},{10,1... | collective-permute-start | bytes 12296 | tf_op jit(solution)/shard_map/ppermute | solution.py:37
  136.8 5.3 %collective-permute-start.27 = (f32[2,512]{1,0:T(2,128)S(1)}, f32[2,512]{1,0:T(2,128)S(1)}, u32[]{:S(2)}, u32[]{:S(2)}) collective-permute-start(f32[2,512]{1,0:T(2,128)S(1)} %pad_maximum_fusion.3), channel_id=1, source_target_pairs={{0,2},{1,3},{2,0},{3,1},{4,6},{5,7},{6,4},{7,5},{8,10},{9,11},{10,... | collective-permute-start | bytes 12296 | tf_op jit(solution)/shard_map/ppermute | solution.py:37
  140.5 3.6 %collective-permute-start.28 = (f32[2,512]{1,0:T(2,128)S(1)}, f32[2,512]{1,0:T(2,128)S(1)}, u32[]{:S(2)}, u32[]{:S(2)}) collective-permute-start(f32[2,512]{1,0:T(2,128)S(1)} %pad_maximum_fusion.3), channel_id=1, source_target_pairs={{0,3},{1,0},{2,1},{3,2},{4,7},{5,4},{6,5},{7,6},{8,11},{9,8},{10,9... | collective-permute-start | bytes 12296 | tf_op jit(solution)/shard_map/ppermute | solution.py:37
  144.2 5.2 %collective-permute-start.29 = (f32[2,512]{1,0:T(2,128)S(1)}, f32[2,512]{1,0:T(2,128)S(1)}, u32[]{:S(2)}, u32[]{:S(2)}) collective-permute-start(f32[2,512]{1,0:T(2,128)S(1)} %pad_maximum_fusion.4), channel_id=1, source_target_pairs={{0,4},{4,0},{1,5},{5,1},{2,6},{6,2},{3,7},{7,3},{8,12},{12,8},{9,1... | collective-permute-start | bytes 12296 | tf_op jit(solution)/shard_map/ppermute | solution.py:37
where the time goes:
time: 151 us
  Pallas kernels  63.9 us (42%)
  starting transfers between devices  53.3 us (35%)
  waiting for transfers between devices  23.5 us (16%)
  other arithmetic  5.69 us (4%)
  local copies, waits for them, and re-layouts  3.59 us (2%)
    ppermute x30, starting transfers between devices, move(): return lax.ppermute(value, axes, pairs)  41.7 us
    ppermute x30, waiting for transfers between devices, move(): return lax.ppermute(value, axes, pairs)  23.5 us
    pallas_call x4, Pallas kernels, project(): pl.pallas_call(functools.partial(project_kernel, far, ordered), out_shape...  19.4 us
    pallas_call x1, Pallas kernels, attend_fresh(): pl.pallas_call(fresh_kernel, out_shape=STATE, in_specs=[SMEM, VMEM] + [AN...  13.8 us
    pallas_call x1, Pallas kernels, attend_early(): pl.pallas_call(early_kernel, out_shape=STATE, in_specs=[SMEM, VMEM] + [AN...  10.4 us
    pallas_call x1, Pallas kernels, attend_late(): pl.pallas_call(late_kernel, out_shape=[jax.ShapeDtypeStruct((HALF, HD), j...  9.8 us
    pallas_call x1, Pallas kernels, side(): pl.pallas_call(side_kernel, out_shape=[shape(4, 512, COLS)] + [shape(1024...  7.13 us
    all_to_all x1, starting transfers between devices, shards(): mine = lax.all_to_all(after(part, g1, fq), 'x', 0, 0)  4.8 us
  transfers between devices with their start and end apart: 33, of which 13 were waited for; matrix products, arithmetic and copies ran while one was open for 1% of the time, Pallas kernels for 40%

commit v1 on v0

--- a/solution.py
+++ b/solution.py
@@ -340,6 +340,7 @@
             flops=2_600_000 * 512, bytes_accessed=4 << 20, transcendentals=2_600_000
         ),
         name="attend_fresh",
+        compiler_params=pltpu.CompilerParams(vmem_limit_bytes=67_043_328),
     )(blocks, fq, *fresh, *pools, acc, row)
 
 
@@ -383,6 +384,7 @@
             flops=2_000_000 * 512, bytes_accessed=4 << 20, transcendentals=2_000_000
         ),
         name="attend_late",
+        compiler_params=pltpu.CompilerParams(vmem_limit_bytes=67_043_328),
     )(blocks, fq, *pools, acc, row)
 
 
@@ -438,6 +440,7 @@
             flops=2 * HALF * 2048 * COLS, bytes_accessed=5 << 20, transcendentals=0
         ),
         name=f"project{ordered}_" + ("far" if far else "near"),
+        compiler_params=pltpu.CompilerParams(vmem_limit_bytes=67_043_328),
     )(*pieces, *weights)
 
 

time: 151 us -> 152 us (level)
  the two profiles are of different devices: /device:TPU:0 before, /device:TPU:32 now
where the time goes in v1:
time: 152 us
  Pallas kernels  65.8 us (43%)
  starting transfers between devices  52 us (34%)
  waiting for transfers between devices  21.4 us (14%)
  other arithmetic  7.1 us (5%)
  local copies, waits for them, and re-layouts  4.44 us (3%)
    ppermute x30, starting transfers between devices, move(): return lax.ppermute(value, axes, pairs)  39.7 us
    ppermute x30, waiting for transfers between devices, move(): return lax.ppermute(value, axes, pairs)  21.4 us
    pallas_call x4, Pallas kernels, project(): pl.pallas_call(functools.partial(project_kernel, far, ordered), out_shape...  19.3 us
    pallas_call x1, Pallas kernels, attend_fresh(): pl.pallas_call(fresh_kernel, out_shape=STATE, in_specs=[SMEM, VMEM] + [AN...  13.8 us
    pallas_call x1, Pallas kernels, attend_early(): pl.pallas_call(early_kernel, out_shape=STATE, in_specs=[SMEM, VMEM] + [AN...  12.5 us
    pallas_call x1, Pallas kernels, attend_late(): pl.pallas_call(late_kernel, out_shape=[jax.ShapeDtypeStruct((HALF, HD), j...  9.79 us
    pallas_call x1, Pallas kernels, side(): pl.pallas_call(side_kernel, out_shape=[shape(4, 512, COLS)] + [shape(1024...  7.13 us
    all_to_all x1, starting transfers between devices, shards(): mine = lax.all_to_all(after(part, g1, fq), 'x', 0, 0)  4.77 us
  transfers between devices with their start and end apart: 33, of which 11 were waited for; matrix products, arithmetic and copies ran while one was open for 4% of the time, Pallas kernels for 41%

profile of v1, /device:TPU:32, one launch (start us, length us, event | category | flops | bytes accessed | tf_op | source)
XLA Modules:
  0.0 151.8 jit_solution(1863231346651016361)
XLA Ops:
  0.6 3.4 %prep.1 = (bf16[4,512,128]{2,1,0:T(8,128)(2,1)}, bf16[2,512,128]{2,1,0:T(8,128)(2,1)}, bf16[2,512,128]{2,1,0:T(8,128)(2,1)}, bf16[2,2,512,128]{3,2,1,0:T(8,128)(2,1)}) custom-call(s32[4,16]{1,0:T(4,128)} %free.3, bf16[512,512]{1,0:T(8,128)(2,1)} %q.1, bf16[1024,512]{1,0:T(8,128)(2,1)} %pk.3, bf16[1024,512]{1,0:T(8,128)(2,1)} %pv.3), custom_call_target="tpu_custom_call" | custom-call | bytes 4194304 | tf_op jit(solution)/shard_map/prep/pallas_call | solution.py:113
  4.0 1.7 %collective-permute-start = (bf16[2,2,512,128]{3,2,1,0:T(8,128)(2,1)}, bf16[2,2,512,128]{3,2,1,0:T(8,128)(2,1)S(1)}, u32[]{:S(2)}, u32[]{:S(2)}) collective-permute-start(bf16[2,2,512,128]{3,2,1,0:T(8,128)(2,1)} %get-tuple-element.34), channel_id=1, source_target_pairs={{0,16},{16,0},{1,17},{17,1},{2,18},{18,2},{3,19},{19,3},{4,20},{20... | collective-permute-start | bytes 1572872 | tf_op jit(solution)/shard_map/ppermute | solution.py:37
  5.7 3.5 %all-to-all-start = ((bf16[4,512,128]{2,1,0:T(8,128)(2,1)}), bf16[4,512,128]{2,1,0:T(8,128)(2,1)S(1)}, u32[]{:S(2)}, u32[]{:S(2)}) async-start(bf16[4,512,128]{2,1,0:T(8,128)(2,1)} %get-tuple-element.37), calls=%async_computation | async-start | bytes 1048576 | tf_op jit(solution)/shard_map/all_to_all | solution.py:461
  9.2 1.0 pad_maximum_fusion.g0
  10.2 3.5 %collective-permute-start.2 = (bf16[2,2,512,128]{3,2,1,0:T(8,128)(2,1)S(1)}, bf16[2,2,512,128]{3,2,1,0:T(8,128)(2,1)}, u32[]{:S(2)}, u32[]{:S(2)}) collective-permute-start(bf16[2,2,512,128]{3,2,1,0:T(8,128)(2,1)S(1)} %pad_maximum_fusion.g0), channel_id=1, source_target_pairs={{0,48},{16,32},{32,16},{48,0},{1,49},{17,33},{33,17},{49,1},{2,50}... | collective-permute-start | bytes 1572872 | tf_op jit(solution)/shard_map/ppermute | solution.py:37
  13.7 0.1 collective-permute-start.4
  13.8 5.3 %collective-permute-done = bf16[2,2,512,128]{3,2,1,0:T(8,128)(2,1)S(1)} collective-permute-done((bf16[2,2,512,128]{3,2,1,0:T(8,128)(2,1)}, bf16[2,2,512,128]{3,2,1,0:T(8,128)(2,1)S(1)}, u32[]{:S(2)}, u32[]{:S(2)}) %collective-permute-start) | collective-permute-done | bytes 524320 | tf_op jit(solution)/shard_map/ppermute | solution.py:37
  19.2 7.1 %side.1 = (bf16[4,512,896]{2,1,0:T(8,128)(2,1)}, bf16[1024,512]{1,0:T(8,128)(2,1)}, bf16[1024,512]{1,0:T(8,128)(2,1)}, bf16[2,512,128]{2,1,0:T(8,128)(2,1)}, bf1...) custom-call(s32[1]{0:T(128)} %constant.4.clone.1.gate, ...), custom_call_target="tpu_custom_call" | custom-call | bytes 14680064 | tf_op jit(solution)/shard_map/side/pallas_call | solution.py:186
  26.5 0.9 collective-permute-done.4.z0
  27.4 0.8 copy-done.12
  28.2 0.2 copy-done.5
  28.3 4.8 %all-to-all-start.1 = ((bf16[4,512,896]{2,1,0:T(8,128)(2,1)}), bf16[4,512,896]{2,1,0:T(8,128)(2,1)}, u32[]{:S(2)}, u32[]{:S(2)}) async-start(bf16[4,512,896]{2,1,0:T(8,128)(2,1)} %get-tuple-element.59), calls=%async_computation.1 | async-start | bytes 7340032 | tf_op jit(solution)/shard_map/all_to_all | solution.py:477
  33.1 0.4 collective-permute-start.6
  33.5 0.6 collective-permute-start.9
  34.1 2.2 %collective-permute-start.11 = (bf16[2,2,512,128]{3,2,1,0:T(8,128)(2,1)S(1)}, bf16[2,2,512,128]{3,2,1,0:T(8,128)(2,1)S(1)}, u32[]{:S(2)}, u32[]{:S(2)}) collective-permute-start(bf16[2,2,512,128]{3,2,1,0:T(8,128)(2,1)S(1)} %pad_maximum_fusion.1.g1), channel_id=1, source_target_pairs={{0,48},{16,32},{32,16},{48,0},{1,49},{17,33},{33,17},{49,1},{2,50}... | collective-permute-start | bytes 1572872 | tf_op jit(solution)/shard_map/ppermute | solution.py:37
  36.3 1.9 %collective-permute-start.5 = (bf16[2,2,512,128]{3,2,1,0:T(8,128)(2,1)}, bf16[2,2,512,128]{3,2,1,0:T(8,128)(2,1)}, u32[]{:S(2)}, u32[]{:S(2)}) collective-permute-start(bf16[2,2,512,128]{3,2,1,0:T(8,128)(2,1)} %collective-permute-done.2.y0), channel_id=1, source_target_pairs={{0,64},{64,0},{1,65},{65,1},{2,66},{66,2},{3,67},{67,3},{4,68},{68... | collective-permute-start | bytes 1572872 | tf_op jit(solution)/shard_map/ppermute | solution.py:37
  38.2 12.5 %attend_early.1 = (f32[128,2048]{1,0:T(8,128)}, f32[8,2048]{1,0:T(8,128)}) custom-call(s32[40]{0:T(128)} %get-tuple-element.42.blocks, bf16[4,512,128]{2,1,0:T(8,128)(2,1)} %copy-done.5, bf16[2,2,512,128]{3,2,1,0:T(8,128)(2,1)} %copy-done.6, bf16[2,2,512,128]{3,2,1,0:T(8,128)(2,1)} %copy-done.7, bf16[2,2,512,128]{3,2,1,0:T(8,128)(2,1)} %collective-permute-done.2.y0, ...), custom_call_target="tpu_custom_call" | custom-call | flops 2048000000 | bytes 4194304 | tf_op jit(solution)/shard_map/attend_early/pallas_call | solution.py:281
  50.7 0.1 collective-permute-start.7
  50.8 0.5 collective-permute-start.10
  51.3 1.3 collective-permute-done.10.f3
  52.6 0.7 copy-done.17
  53.3 13.8 %attend_fresh.1 = (f32[128,2048]{1,0:T(8,128)}, f32[8,2048]{1,0:T(8,128)}) custom-call(s32[40]{0:T(128)} %get-tuple-element.45.blocks, bf16[4,512,128]{2,1,0:T(8,128)(2,1)} %copy-done.5, bf16[2,512,128]{2,1,0:T(8,128)(2,1)} %get-tuple-element.46.f0, bf16[2,512,128]{2,1,0:T(8,128)(2,1)} %copy-done.16, bf16[2,2,512,128]{3,2,1,0:T(8,128)(2,1)} %copy-done.8, ...), custom_call_target="tpu_custom_call" | custom-call | flops 1331200000 | bytes 4194304 | tf_op jit(solution)/shard_map/attend_fresh/pallas_call | solution.py:329
  67.1 9.8 %attend_late.1 = (bf16[256,128]{1,0:T(8,128)(2,1)}, bf16[256,128]{1,0:T(8,128)(2,1)}, bf16[256,128]{1,0:T(8,128)(2,1)}, bf16[256,128]{1,0:T(8,128)(2,1)}, bf16[4,256,128]{2,1,0:T(8,128)(2,1)}) custom-call(s32[40]{0:T(128)} %get-tuple-element.36.blocks, bf16[4,512,128]{2,1,0:T(8,128)(2,1)} %copy-done.5, bf16[2,2,512,128]{3,2,1,0:T(8,128)(2,1)} %collective-permute-done.5.d0, ...), custom_call_target="tpu_custom_call" | custom-call | flops 1024000000 | bytes 4194304 | tf_op jit(solution)/shard_map/attend_late/pallas_call | solution.py:371
  76.9 0.5 collective-permute-start.12
  77.5 0.7 collective-permute-start.13
  78.2 0.9 collective-permute-start.14
  79.1 3.4 %collective-permute-done.13 = bf16[256,128]{1,0:T(8,128)(2,1)S(1)} collective-permute-done((bf16[256,128]{1,0:T(8,128)(2,1)}, bf16[256,128]{1,0:T(8,128)(2,1)S(1)}, u32[]{:S(2)}, u32[]{:S(2)}) %collective-permute-start.13) | collective-permute-done | bytes 65568 | tf_op jit(solution)/shard_map/ppermute | solution.py:37
  82.6 0.2 collective-permute-done.14
  82.8 0.9 pad_maximum_fusion.2.a0
  83.7 0.5 collective-permute-start.19
  84.2 1.9 %collective-permute-start.15 = (bf16[4,256,128]{2,1,0:T(8,128)(2,1)S(1)}, bf16[4,256,128]{2,1,0:T(8,128)(2,1)S(1)}, u32[]{:S(2)}, u32[]{:S(2)}) collective-permute-start(bf16[4,256,128]{2,1,0:T(8,128)(2,1)S(1)} %pad_maximum_fusion.2.a0), channel_id=1, source_target_pairs={{0,1},{1,2},{2,3},{3,0},{4,5},{5,6},{6,7},{7,4},{8,9},{9,10},{10,1... | collective-permute-start | bytes 786440 | tf_op jit(solution)/shard_map/ppermute | solution.py:37
  86.1 1.4 collective-permute-start.16
  87.4 4.0 %all-to-all-start.2 = ((bf16[4,256,128]{2,1,0:T(8,128)(2,1)}), bf16[4,256,128]{2,1,0:T(8,128)(2,1)}, u32[]{:S(2)}, u32[]{:S(2)}) async-start(bf16[4,256,128]{2,1,0:T(8,128)(2,1)} %get-tuple-element.61), calls=%async_computation.2 | async-start | bytes 524288 | tf_op jit(solution)/shard_map/all_to_all | solution.py:487
  91.5 2.4 %collective-permute-done.15.ap = bf16[4,256,128]{2,1,0:T(8,128)(2,1)S(1)} collective-permute-done((bf16[4,256,128]{2,1,0:T(8,128)(2,1)S(1)}, bf16[4,256,128]{2,1,0:T(8,128)(2,1)S(1)}, u32[]{:S(2)}, u32[]{:S(2)}) %collective-permute-start.15) | collective-permute-done | bytes 262176 | tf_op jit(solution)/shard_map/ppermute | solution.py:37
  93.9 0.6 collective-permute-start.17
  94.4 0.1 copy-done.3
  94.6 0.7 copy-done.4
  95.3 2.7 %collective-permute-start.18 = (bf16[2,256,128]{2,1,0:T(8,128)(2,1)S(1)}, bf16[2,256,128]{2,1,0:T(8,128)(2,1)}, u32[]{:S(2)}, u32[]{:S(2)}) collective-permute-start(bf16[2,256,128]{2,1,0:T(8,128)(2,1)S(1)} %slice.68), channel_id=1, source_target_pairs={{0,3},{1,0},{2,1},{3,2},{4,7},{5,4},{6,5},{7,6},{8,11},{9,8},{10,9... | collective-permute-start | bytes 393224 | tf_op jit(solution)/shard_map/ppermute | solution.py:37
  98.0 0.2 collective-permute-start.21
  98.2 3.0 %collective-permute-start.22 = (bf16[4,256,128]{2,1,0:T(8,128)(2,1)}, bf16[4,256,128]{2,1,0:T(8,128)(2,1)}, u32[]{:S(2)}, u32[]{:S(2)}) collective-permute-start(bf16[4,256,128]{2,1,0:T(8,128)(2,1)} %all-to-all-done.2.a0), channel_id=1, source_target_pairs={{0,3},{1,0},{2,1},{3,2},{4,7},{5,4},{6,5},{7,6},{8,11},{9,8},{10,9... | collective-permute-start | bytes 786440 | tf_op jit(solution)/shard_map/ppermute | solution.py:37
  101.3 4.8 %project0_far.1 = bf16[256,896]{1,0:T(8,128)(2,1)} custom-call(bf16[4,256,128]{2,1,0:T(8,128)(2,1)} %copy-done.2, bf16[4,256,128]{2,1,0:T(8,128)(2,1)} %copy-done.3, bf16[4,256,128]{2,1,0:T(8,128)(2,1)} %copy-done.4, bf16[2,256,128]{2,1,0:T(8,128)(2,1)} %collective-permute-done.17.a2a, bf16[2,256,128]{2,1,0:T(8,128)(2,1)} %collective-permute-done.18.a2b, ...), custom_call_target="tpu_custom_call" | custom-call | flops 939524096 | bytes 5242880 | tf_op jit(solution)/shard_map/project0_far/pallas_call | solution.py:429
  106.1 3.0 %collective-permute-start.20 = (bf16[256,896]{1,0:T(8,128)(2,1)}, bf16[256,896]{1,0:T(8,128)(2,1)}, u32[]{:S(2)}, u32[]{:S(2)}) collective-permute-start(bf16[256,896]{1,0:T(8,128)(2,1)} %project0_far.1), channel_id=1, source_target_pairs={{0,4},{4,0},{1,5},{5,1},{2,6},{6,2},{3,7},{7,3},{8,12},{12,8},{9,1... | collective-permute-start | bytes 1376264 | tf_op jit(solution)/shard_map/ppermute | solution.py:37
  109.1 0.9 slice.69
  110.0 0.5 collective-permute-start.23
  110.5 0.9 slice.70
  111.4 2.9 %collective-permute-start.24 = (bf16[2,256,128]{2,1,0:T(8,128)(2,1)S(1)}, bf16[2,256,128]{2,1,0:T(8,128)(2,1)}, u32[]{:S(2)}, u32[]{:S(2)}) collective-permute-start(bf16[2,256,128]{2,1,0:T(8,128)(2,1)S(1)} %slice.70), channel_id=1, source_target_pairs={{0,3},{1,0},{2,1},{3,2},{4,7},{5,4},{6,5},{7,6},{8,11},{9,8},{10,9... | collective-permute-start | bytes 393224 | tf_op jit(solution)/shard_map/ppermute | solution.py:37
  114.3 2.1 %collective-permute-done.23.a2a = bf16[2,256,128]{2,1,0:T(8,128)(2,1)} collective-permute-done((bf16[2,256,128]{2,1,0:T(8,128)(2,1)S(1)}, bf16[2,256,128]{2,1,0:T(8,128)(2,1)}, u32[]{:S(2)}, u32[]{:S(2)}) %collective-permute-start.23) | collective-permute-done | bytes 131104 | tf_op jit(solution)/shard_map/ppermute | solution.py:37
  116.4 0.5 collective-permute-done.24.a2b
  116.8 4.7 %project1_far.1 = bf16[256,896]{1,0:T(8,128)(2,1)} custom-call(bf16[4,256,128]{2,1,0:T(8,128)(2,1)} %all-to-all-done.2.a0, bf16[4,256,128]{2,1,0:T(8,128)(2,1)} %collective-permute-done.21.ap, bf16[4,256,128]{2,1,0:T(8,128)(2,1)} %collective-permute-done.22.am, bf16[2,256,128]{2,1,0:T(8,128)(2,1)} %collective-permute-done.23.a2a, ...), custom_call_target="tpu_custom_call" | custom-call | flops 939524096 | bytes 5242880 | tf_op jit(solution)/shard_map/project1_far/pallas_call | solution.py:429
  121.6 1.1 collective-permute-start.25
  122.6 4.8 %project0_near.1 = f32[256,896]{1,0:T(8,128)} custom-call(bf16[4,256,128]{2,1,0:T(8,128)(2,1)} %copy-done.2, bf16[4,256,128]{2,1,0:T(8,128)(2,1)} %copy-done.3, bf16[4,256,128]{2,1,0:T(8,128)(2,1)} %copy-done.4, bf16[2,256,128]{2,1,0:T(8,128)(2,1)} %collective-permute-done.17.a2a, bf16[2,256,128]{2,1,0:T(8,128)(2,1)} %collective-permute-done.18.a2b, ...), custom_call_target="tpu_custom_call" | custom-call | flops 939524096 | bytes 5242880 | tf_op jit(solution)/shard_map/project0_near/pallas_call | solution.py:429
  127.5 4.9 %project1_near.1 = f32[256,896]{1,0:T(8,128)} custom-call(bf16[4,256,128]{2,1,0:T(8,128)(2,1)} %all-to-all-done.2.a0, bf16[4,256,128]{2,1,0:T(8,128)(2,1)} %collective-permute-done.21.ap, bf16[4,256,128]{2,1,0:T(8,128)(2,1)} %collective-permute-done.22.am, bf16[2,256,128]{2,1,0:T(8,128)(2,1)} %collective-permute-done.23.a2a, ...), custom_call_target="tpu_custom_call" | custom-call | flops 939524096 | bytes 5242880 | tf_op jit(solution)/shard_map/project1_near/pallas_call | solution.py:429
  132.4 1.5 convert_add_fusion.1
  134.0 1.1 convert_add_fusion
  135.1 0.3 fusion.1
  135.5 0.5 multiply_reduce_fusion
  135.9 1.4 collective-permute-start.26
  137.4 3.8 %collective-permute-start.27 = (f32[2,512]{1,0:T(2,128)S(1)}, f32[2,512]{1,0:T(2,128)S(1)}, u32[]{:S(2)}, u32[]{:S(2)}) collective-permute-start(f32[2,512]{1,0:T(2,128)S(1)} %pad_maximum_fusion.3), channel_id=1, source_target_pairs={{0,2},{1,3},{2,0},{3,1},{4,6},{5,7},{6,4},{7,5},{8,10},{9,11},{10,... | collective-permute-start | bytes 12296 | tf_op jit(solution)/shard_map/ppermute | solution.py:37
  141.2 0.9 collective-permute-start.28
  142.1 0.8 collective-permute-done.27
  142.8 2.0 %collective-permute-done.28 = f32[2,512]{1,0:T(2,128)S(1)} collective-permute-done((f32[2,512]{1,0:T(2,128)S(1)}, f32[2,512]{1,0:T(2,128)S(1)}, u32[]{:S(2)}, u32[]{:S(2)}) %collective-permute-start.28) | collective-permute-done | bytes 4128 | tf_op jit(solution)/shard_map/ppermute | solution.py:37
  144.9 2.6 %collective-permute-start.29 = (f32[2,512]{1,0:T(2,128)S(1)}, f32[2,512]{1,0:T(2,128)S(1)}, u32[]{:S(2)}, u32[]{:S(2)}) collective-permute-start(f32[2,512]{1,0:T(2,128)S(1)} %pad_maximum_fusion.4), channel_id=1, source_target_pairs={{0,4},{4,0},{1,5},{5,1},{2,6},{6,2},{3,7},{7,3},{8,12},{12,8},{9,1... | collective-permute-start | bytes 12296 | tf_op jit(solution)/shard_map/ppermute | solution.py:37
  147.5 2.6 %collective-permute-done.29 = f32[2,512]{1,0:T(2,128)S(1)} collective-permute-done((f32[2,512]{1,0:T(2,128)S(1)}, f32[2,512]{1,0:T(2,128)S(1)}, u32[]{:S(2)}, u32[]{:S(2)}) %collective-permute-start.29) | collective-permute-done | bytes 4128 | tf_op jit(solution)/shard_map/ppermute | solution.py:37
  150.1 1.7 %add_convert_fusion = (bf16[512,896]{1,0:T(8,128)(2,1)}, bf16[512,896]{1,0:T(8,128)(2,1)}) fusion(f32[896]{0:T(1024)S(1)} %copy-done.10, f32[896]{0:T(1024)S(1)} %copy-done.11, f32[512]{0:T(512)S(1)} %get-tuple-element.71, f32[512]{0:T(512)S(1)} %get-tuple-element.70, f32[896]{0:T(1024)S(1)} %copy-done.9, f32[256,896]{1,0:T(8,128)S(1)} %convert_add_fusion, ...), kind=kLoop, calls=%fused_computation.2 | loop fusion | flops 4587520 | bytes 4602368 | tf_op jit(solution)/shard_map/convert_element_type | solution.py:508
  (67 shorter events, 0.5 us)
Async XLA Ops:
  4.0 15.1 %collective-permute-start = (bf16[2,2,512,128]{3,2,1,0:T(8,128)(2,1)}, bf16[2,2,512,128]{3,2,1,0:T(8,128)(2,1)S(1)}, u32[]{:S(2)}, u32[]{:S(2)}) collective-permute-start(bf16[2,2,512,128]{3,2,1,0:T(8,128)(2,1)} %get-tuple-element.34), channel_id=1, source_target_pairs={{0,16},{16,0},{1,17},{17,1},{2,18},{18,2},{3,19},{19,3},{4,20},{20... | collective-permute-start | bytes 1572872 | tf_op jit(solution)/shard_map/ppermute | solution.py:37
  5.7 3.5 %collective-permute-start.1 = (bf16[2,512,128]{2,1,0:T(8,128)(2,1)}, bf16[2,512,128]{2,1,0:T(8,128)(2,1)S(1)}, u32[]{:S(2)}, u32[]{:S(2)}) collective-permute-start(bf16[2,512,128]{2,1,0:T(8,128)(2,1)} %get-tuple-element.39), channel_id=1, source_target_pairs={{0,8},{8,0},{1,9},{9,1},{2,10},{10,2},{3,11},{11,3},{4,12},{12,4},... | collective-permute-start | bytes 786440 | tf_op jit(solution)/shard_map/ppermute | solution.py:37
  5.7 21.7 %all-to-all-start = ((bf16[4,512,128]{2,1,0:T(8,128)(2,1)}), bf16[4,512,128]{2,1,0:T(8,128)(2,1)S(1)}, u32[]{:S(2)}, u32[]{:S(2)}) async-start(bf16[4,512,128]{2,1,0:T(8,128)(2,1)} %get-tuple-element.37), calls=%async_computation | async-start | bytes 1048576 | tf_op jit(solution)/shard_map/all_to_all | solution.py:461
  10.2 16.2 %copy-start.6 = (bf16[2,2,512,128]{3,2,1,0:T(8,128)(2,1)}, bf16[2,2,512,128]{3,2,1,0:T(8,128)(2,1)S(1)}, u32[]{:S(2)}) copy-start(bf16[2,2,512,128]{3,2,1,0:T(8,128)(2,1)S(1)} %pad_maximum_fusion.g0) | copy-start | bytes 1572868
  10.2 16.3 %collective-permute-start.2 = (bf16[2,2,512,128]{3,2,1,0:T(8,128)(2,1)S(1)}, bf16[2,2,512,128]{3,2,1,0:T(8,128)(2,1)}, u32[]{:S(2)}, u32[]{:S(2)}) collective-permute-start(bf16[2,2,512,128]{3,2,1,0:T(8,128)(2,1)S(1)} %pad_maximum_fusion.g0), channel_id=1, source_target_pairs={{0,48},{16,32},{32,16},{48,0},{1,49},{17,33},{33,17},{49,1},{2,50}... | collective-permute-start | bytes 1572872 | tf_op jit(solution)/shard_map/ppermute | solution.py:37
  13.7 13.7 %collective-permute-start.4 = (bf16[2,2,512,128]{3,2,1,0:T(8,128)(2,1)S(1)}, bf16[2,2,512,128]{3,2,1,0:T(8,128)(2,1)S(1)}, u32[]{:S(2)}, u32[]{:S(2)}) collective-permute-start(bf16[2,2,512,128]{3,2,1,0:T(8,128)(2,1)S(1)} %pad_maximum_fusion.g0), channel_id=1, source_target_pairs={{0,64},{64,0},{1,65},{65,1},{2,66},{66,2},{3,67},{67,3},{4,68},{68... | collective-permute-start | bytes 1572872 | tf_op jit(solution)/shard_map/ppermute | solution.py:37
  19.2 7.2 %collective-permute-start.3 = (bf16[2,512,128]{2,1,0:T(8,128)(2,1)S(1)}, bf16[2,512,128]{2,1,0:T(8,128)(2,1)S(1)}, u32[]{:S(2)}, u32[]{:S(2)}) collective-permute-start(bf16[2,512,128]{2,1,0:T(8,128)(2,1)S(1)} %get-tuple-element.69), channel_id=1, source_target_pairs={{0,8},{8,0},{1,9},{9,1},{2,10},{10,2},{3,11},{11,3},{4,12},{12,4},... | collective-permute-start | bytes 786440 | tf_op jit(solution)/shard_map/ppermute | solution.py:37
  26.5 7.6 %copy-start.7 = (bf16[2,2,512,128]{3,2,1,0:T(8,128)(2,1)}, bf16[2,2,512,128]{3,2,1,0:T(8,128)(2,1)S(1)}, u32[]{:S(2)}) copy-start(bf16[2,2,512,128]{3,2,1,0:T(8,128)(2,1)S(1)} %pad_maximum_fusion.1.g1) | copy-start | bytes 1572868
  27.4 0.8 copy-start.12
  27.4 1.0 copy-start.5
  27.4 6.1 %copy-start.13 = (bf16[2,2,512,128]{3,2,1,0:T(8,128)(2,1)S(1)}, bf16[2,2,512,128]{3,2,1,0:T(8,128)(2,1)}, u32[]{:S(2)}) copy-start(bf16[2,2,512,128]{3,2,1,0:T(8,128)(2,1)} %get-tuple-element.50) | copy-start | bytes 1572868
  27.4 8.9 %copy-start.15 = (bf16[2,512,128]{2,1,0:T(8,128)(2,1)S(1)}, bf16[2,512,128]{2,1,0:T(8,128)(2,1)}, u32[]{:S(2)}) copy-start(bf16[2,512,128]{2,1,0:T(8,128)(2,1)} %get-tuple-element.48) | copy-start | bytes 786436
  28.3 55.3 %all-to-all-start.1 = ((bf16[4,512,896]{2,1,0:T(8,128)(2,1)}), bf16[4,512,896]{2,1,0:T(8,128)(2,1)}, u32[]{:S(2)}, u32[]{:S(2)}) async-start(bf16[4,512,896]{2,1,0:T(8,128)(2,1)} %get-tuple-element.59), calls=%async_computation.1 | async-start | bytes 7340032 | tf_op jit(solution)/shard_map/all_to_all | solution.py:477
  33.1 17.5 %collective-permute-start.6 = (bf16[2,2,512,128]{3,2,1,0:T(8,128)(2,1)S(1)}, bf16[2,2,512,128]{3,2,1,0:T(8,128)(2,1)}, u32[]{:S(2)}, u32[]{:S(2)}) collective-permute-start(bf16[2,2,512,128]{3,2,1,0:T(8,128)(2,1)S(1)} %pad_maximum_fusion.1.g1), channel_id=1, source_target_pairs={{0,64},{64,0},{1,65},{65,1},{2,66},{66,2},{3,67},{67,3},{4,68},{68... | collective-permute-start | bytes 1572872 | tf_op jit(solution)/shard_map/ppermute | solution.py:37
  33.5 17.3 %collective-permute-start.9 = (bf16[2,2,512,128]{3,2,1,0:T(8,128)(2,1)S(1)}, bf16[2,2,512,128]{3,2,1,0:T(8,128)(2,1)S(1)}, u32[]{:S(2)}, u32[]{:S(2)}) collective-permute-start(bf16[2,2,512,128]{3,2,1,0:T(8,128)(2,1)S(1)} %copy-done.13), channel_id=1, source_target_pairs={{0,16},{16,0},{1,17},{17,1},{2,18},{18,2},{3,19},{19,3},{4,20},{20... | collective-permute-start | bytes 1572872 | tf_op jit(solution)/shard_map/ppermute | solution.py:37
  34.1 17.2 %collective-permute-start.11 = (bf16[2,2,512,128]{3,2,1,0:T(8,128)(2,1)S(1)}, bf16[2,2,512,128]{3,2,1,0:T(8,128)(2,1)S(1)}, u32[]{:S(2)}, u32[]{:S(2)}) collective-permute-start(bf16[2,2,512,128]{3,2,1,0:T(8,128)(2,1)S(1)} %pad_maximum_fusion.1.g1), channel_id=1, source_target_pairs={{0,48},{16,32},{32,16},{48,0},{1,49},{17,33},{33,17},{49,1},{2,50}... | collective-permute-start | bytes 1572872 | tf_op jit(solution)/shard_map/ppermute | solution.py:37
  36.3 15.0 %collective-permute-start.8 = (bf16[2,512,128]{2,1,0:T(8,128)(2,1)S(1)}, bf16[2,512,128]{2,1,0:T(8,128)(2,1)S(1)}, u32[]{:S(2)}, u32[]{:S(2)}) collective-permute-start(bf16[2,512,128]{2,1,0:T(8,128)(2,1)S(1)} %copy-done.15), channel_id=1, source_target_pairs={{0,8},{8,0},{1,9},{9,1},{2,10},{10,2},{3,11},{11,3},{4,12},{12,4},... | collective-permute-start | bytes 786440 | tf_op jit(solution)/shard_map/ppermute | solution.py:37
  36.3 30.9 %collective-permute-start.5 = (bf16[2,2,512,128]{3,2,1,0:T(8,128)(2,1)}, bf16[2,2,512,128]{3,2,1,0:T(8,128)(2,1)}, u32[]{:S(2)}, u32[]{:S(2)}) collective-permute-start(bf16[2,2,512,128]{3,2,1,0:T(8,128)(2,1)} %collective-permute-done.2.y0), channel_id=1, source_target_pairs={{0,64},{64,0},{1,65},{65,1},{2,66},{66,2},{3,67},{67,3},{4,68},{68... | collective-permute-start | bytes 1572872 | tf_op jit(solution)/shard_map/ppermute | solution.py:37
  50.7 16.5 %collective-permute-start.7 = (bf16[2,2,512,128]{3,2,1,0:T(8,128)(2,1)}, bf16[2,2,512,128]{3,2,1,0:T(8,128)(2,1)}, u32[]{:S(2)}, u32[]{:S(2)}) collective-permute-start(bf16[2,2,512,128]{3,2,1,0:T(8,128)(2,1)} %collective-permute-done.6.z1), channel_id=1, source_target_pairs={{0,48},{16,32},{32,16},{48,0},{1,49},{17,33},{33,17},{49,1},{2,50}... | collective-permute-start | bytes 1572872 | tf_op jit(solution)/shard_map/ppermute | solution.py:37
  50.8 1.8 %copy-start.8 = (bf16[2,2,512,128]{3,2,1,0:T(8,128)(2,1)}, bf16[2,2,512,128]{3,2,1,0:T(8,128)(2,1)S(1)}, u32[]{:S(2)}) copy-start(bf16[2,2,512,128]{3,2,1,0:T(8,128)(2,1)S(1)} %collective-permute-done.9.fy) | copy-start | bytes 1572868
  50.8 1.8 %collective-permute-start.10 = (bf16[2,512,128]{2,1,0:T(8,128)(2,1)S(1)}, bf16[2,512,128]{2,1,0:T(8,128)(2,1)S(1)}, u32[]{:S(2)}, u32[]{:S(2)}) collective-permute-start(bf16[2,512,128]{2,1,0:T(8,128)(2,1)S(1)} %slice_bitcast_fusion), channel_id=1, source_target_pairs={{0,8},{8,0},{1,9},{9,1},{2,10},{10,2},{3,11},{11,3},{4,12},{12,4},... | collective-permute-start | bytes 786440 | tf_op jit(solution)/shard_map/ppermute | solution.py:37
  51.3 1.3 copy-start.16
  51.3 1.3 copy-start.14
  52.6 0.7 copy-start.17
  76.9 2.2 %collective-permute-start.12 = (bf16[256,128]{1,0:T(8,128)(2,1)}, bf16[256,128]{1,0:T(8,128)(2,1)S(1)}, u32[]{:S(2)}, u32[]{:S(2)}) collective-permute-start(bf16[256,128]{1,0:T(8,128)(2,1)} %get-tuple-element.55), channel_id=1, source_target_pairs={{0,8},{8,0},{1,9},{9,1},{2,10},{10,2},{3,11},{11,3},{4,12},{12,4},... | collective-permute-start | bytes 196616 | tf_op jit(solution)/shard_map/ppermute | solution.py:37
  77.5 5.1 %collective-permute-start.13 = (bf16[256,128]{1,0:T(8,128)(2,1)}, bf16[256,128]{1,0:T(8,128)(2,1)S(1)}, u32[]{:S(2)}, u32[]{:S(2)}) collective-permute-start(bf16[256,128]{1,0:T(8,128)(2,1)} %get-tuple-element.56), channel_id=1, source_target_pairs={{0,16},{16,0},{1,17},{17,1},{2,18},{18,2},{3,19},{19,3},{4,20},{20... | collective-permute-start | bytes 196616 | tf_op jit(solution)/shard_map/ppermute | solution.py:37
  78.2 4.6 %collective-permute-start.14 = (bf16[256,128]{1,0:T(8,128)(2,1)}, bf16[256,128]{1,0:T(8,128)(2,1)S(1)}, u32[]{:S(2)}, u32[]{:S(2)}) collective-permute-start(bf16[256,128]{1,0:T(8,128)(2,1)} %get-tuple-element.57), channel_id=1, source_target_pairs={{0,24},{8,16},{16,8},{24,0},{1,25},{9,17},{17,9},{25,1},{2,26},{10... | collective-permute-start | bytes 196616 | tf_op jit(solution)/shard_map/ppermute | solution.py:37
  83.6 2.4 %copy-start.2 = (bf16[4,256,128]{2,1,0:T(8,128)(2,1)}, bf16[4,256,128]{2,1,0:T(8,128)(2,1)S(1)}, u32[]{:S(2)}) copy-start(bf16[4,256,128]{2,1,0:T(8,128)(2,1)S(1)} %pad_maximum_fusion.2.a0) | copy-start | bytes 786436
  83.7 17.6 %collective-permute-start.19 = (bf16[4,512,896]{2,1,0:T(8,128)(2,1)}, bf16[4,512,896]{2,1,0:T(8,128)(2,1)}, u32[]{:S(2)}, u32[]{:S(2)}) collective-permute-start(bf16[4,512,896]{2,1,0:T(8,128)(2,1)} %all-to-all-done.1.mine), channel_id=1, source_target_pairs={{0,8},{8,0},{1,9},{9,1},{2,10},{10,2},{3,11},{11,3},{4,12},{12,4},... | collective-permute-start | bytes 11010056 | tf_op jit(solution)/shard_map/ppermute | solution.py:37
  84.2 9.7 %collective-permute-start.15 = (bf16[4,256,128]{2,1,0:T(8,128)(2,1)S(1)}, bf16[4,256,128]{2,1,0:T(8,128)(2,1)S(1)}, u32[]{:S(2)}, u32[]{:S(2)}) collective-permute-start(bf16[4,256,128]{2,1,0:T(8,128)(2,1)S(1)} %pad_maximum_fusion.2.a0), channel_id=1, source_target_pairs={{0,1},{1,2},{2,3},{3,0},{4,5},{5,6},{6,7},{7,4},{8,9},{9,10},{10,1... | collective-permute-start | bytes 786440 | tf_op jit(solution)/shard_map/ppermute | solution.py:37
  86.1 8.4 %collective-permute-start.16 = (bf16[4,256,128]{2,1,0:T(8,128)(2,1)S(1)}, bf16[4,256,128]{2,1,0:T(8,128)(2,1)S(1)}, u32[]{:S(2)}, u32[]{:S(2)}) collective-permute-start(bf16[4,256,128]{2,1,0:T(8,128)(2,1)S(1)} %pad_maximum_fusion.2.a0), channel_id=1, source_target_pairs={{0,3},{1,0},{2,1},{3,2},{4,7},{5,4},{6,5},{7,6},{8,11},{9,8},{10,9... | collective-permute-start | bytes 786440 | tf_op jit(solution)/shard_map/ppermute | solution.py:37
  87.4 10.6 %all-to-all-start.2 = ((bf16[4,256,128]{2,1,0:T(8,128)(2,1)}), bf16[4,256,128]{2,1,0:T(8,128)(2,1)}, u32[]{:S(2)}, u32[]{:S(2)}) async-start(bf16[4,256,128]{2,1,0:T(8,128)(2,1)} %get-tuple-element.61), calls=%async_computation.2 | async-start | bytes 524288 | tf_op jit(solution)/shard_map/all_to_all | solution.py:487
  93.8 0.7 copy-start.3
  93.9 7.4 %collective-permute-start.17 = (bf16[2,256,128]{2,1,0:T(8,128)(2,1)S(1)}, bf16[2,256,128]{2,1,0:T(8,128)(2,1)}, u32[]{:S(2)}, u32[]{:S(2)}) collective-permute-start(bf16[2,256,128]{2,1,0:T(8,128)(2,1)S(1)} %slice.67), channel_id=1, source_target_pairs={{0,1},{1,2},{2,3},{3,0},{4,5},{5,6},{6,7},{7,4},{8,9},{9,10},{10,1... | collective-permute-start | bytes 393224 | tf_op jit(solution)/shard_map/ppermute | solution.py:37
  94.6 0.7 copy-start.4
  95.3 6.0 %collective-permute-start.18 = (bf16[2,256,128]{2,1,0:T(8,128)(2,1)S(1)}, bf16[2,256,128]{2,1,0:T(8,128)(2,1)}, u32[]{:S(2)}, u32[]{:S(2)}) collective-permute-start(bf16[2,256,128]{2,1,0:T(8,128)(2,1)S(1)} %slice.68), channel_id=1, source_target_pairs={{0,3},{1,0},{2,1},{3,2},{4,7},{5,4},{6,5},{7,6},{8,11},{9,8},{10,9... | collective-permute-start | bytes 393224 | tf_op jit(solution)/shard_map/ppermute | solution.py:37
  98.0 11.1 %collective-permute-start.21 = (bf16[4,256,128]{2,1,0:T(8,128)(2,1)}, bf16[4,256,128]{2,1,0:T(8,128)(2,1)}, u32[]{:S(2)}, u32[]{:S(2)}) collective-permute-start(bf16[4,256,128]{2,1,0:T(8,128)(2,1)} %all-to-all-done.2.a0), channel_id=1, source_target_pairs={{0,1},{1,2},{2,3},{3,0},{4,5},{5,6},{6,7},{7,4},{8,9},{9,10},{10,1... | collective-permute-start | bytes 786440 | tf_op jit(solution)/shard_map/ppermute | solution.py:37
  98.2 12.3 %collective-permute-start.22 = (bf16[4,256,128]{2,1,0:T(8,128)(2,1)}, bf16[4,256,128]{2,1,0:T(8,128)(2,1)}, u32[]{:S(2)}, u32[]{:S(2)}) collective-permute-start(bf16[4,256,128]{2,1,0:T(8,128)(2,1)} %all-to-all-done.2.a0), channel_id=1, source_target_pairs={{0,3},{1,0},{2,1},{3,2},{4,7},{5,4},{6,5},{7,6},{8,11},{9,8},{10,9... | collective-permute-start | bytes 786440 | tf_op jit(solution)/shard_map/ppermute | solution.py:37
  106.1 26.4 %collective-permute-start.20 = (bf16[256,896]{1,0:T(8,128)(2,1)}, bf16[256,896]{1,0:T(8,128)(2,1)}, u32[]{:S(2)}, u32[]{:S(2)}) collective-permute-start(bf16[256,896]{1,0:T(8,128)(2,1)} %project0_far.1), channel_id=1, source_target_pairs={{0,4},{4,0},{1,5},{5,1},{2,6},{6,2},{3,7},{7,3},{8,12},{12,8},{9,1... | collective-permute-start | bytes 1376264 | tf_op jit(solution)/shard_map/ppermute | solution.py:37
  110.0 6.4 %collective-permute-start.23 = (bf16[2,256,128]{2,1,0:T(8,128)(2,1)S(1)}, bf16[2,256,128]{2,1,0:T(8,128)(2,1)}, u32[]{:S(2)}, u32[]{:S(2)}) collective-permute-start(bf16[2,256,128]{2,1,0:T(8,128)(2,1)S(1)} %slice.69), channel_id=1, source_target_pairs={{0,1},{1,2},{2,3},{3,0},{4,5},{5,6},{6,7},{7,4},{8,9},{9,10},{10,1... | collective-permute-start | bytes 393224 | tf_op jit(solution)/shard_map/ppermute | solution.py:37
  111.4 5.4 %collective-permute-start.24 = (bf16[2,256,128]{2,1,0:T(8,128)(2,1)S(1)}, bf16[2,256,128]{2,1,0:T(8,128)(2,1)}, u32[]{:S(2)}, u32[]{:S(2)}) collective-permute-start(bf16[2,256,128]{2,1,0:T(8,128)(2,1)S(1)} %slice.70), channel_id=1, source_target_pairs={{0,3},{1,0},{2,1},{3,2},{4,7},{5,4},{6,5},{7,6},{8,11},{9,8},{10,9... | collective-permute-start | bytes 393224 | tf_op jit(solution)/shard_map/ppermute | solution.py:37
  121.6 12.4 %collective-permute-start.25 = (bf16[256,896]{1,0:T(8,128)(2,1)}, bf16[256,896]{1,0:T(8,128)(2,1)}, u32[]{:S(2)}, u32[]{:S(2)}) collective-permute-start(bf16[256,896]{1,0:T(8,128)(2,1)} %project1_far.1), channel_id=1, source_target_pairs={{0,4},{4,0},{1,5},{5,1},{2,6},{6,2},{3,7},{7,3},{8,12},{12,8},{9,1... | collective-permute-start | bytes 1376264 | tf_op jit(solution)/shard_map/ppermute | solution.py:37
  132.4 1.6 %copy-start.1 = (f32[256,896]{1,0:T(8,128)S(1)}, f32[256,896]{1,0:T(8,128)}, u32[]{:S(2)}) copy-start(f32[256,896]{1,0:T(8,128)} %project1_near.1) | copy-start | bytes 2752516
  132.4 2.7 %copy-start = (bf16[512,896]{1,0:T(8,128)(2,1)S(1)}, bf16[512,896]{1,0:T(8,128)(2,1)}, u32[]{:S(2)}) copy-start(bf16[512,896]{1,0:T(8,128)(2,1)} %param.21) | copy-start | bytes 2752516
  132.4 2.7 %copy-start.9 = (f32[896]{0:T(1024)S(1)}, f32[896]{0:T(1024)}, u32[]{:S(2)}) copy-start(f32[896]{0:T(1024)} %param.23) | copy-start | bytes 10756
  135.4 14.6 %copy-start.10 = (f32[896]{0:T(1024)S(1)}, f32[896]{0:T(1024)}, u32[]{:S(2)}) copy-start(f32[896]{0:T(1024)} %param.25) | copy-start | bytes 10756
  135.4 14.6 %copy-start.11 = (f32[896]{0:T(1024)S(1)}, f32[896]{0:T(1024)}, u32[]{:S(2)}) copy-start(f32[896]{0:T(1024)} %param.24) | copy-start | bytes 10756
  135.9 6.1 %collective-permute-start.26 = (f32[2,512]{1,0:T(2,128)S(1)}, f32[2,512]{1,0:T(2,128)S(1)}, u32[]{:S(2)}, u32[]{:S(2)}) collective-permute-start(f32[2,512]{1,0:T(2,128)S(1)} %pad_maximum_fusion.3), channel_id=1, source_target_pairs={{0,1},{1,2},{2,3},{3,0},{4,5},{5,6},{6,7},{7,4},{8,9},{9,10},{10,1... | collective-permute-start | bytes 12296 | tf_op jit(solution)/shard_map/ppermute | solution.py:37
  137.4 5.4 %collective-permute-start.27 = (f32[2,512]{1,0:T(2,128)S(1)}, f32[2,512]{1,0:T(2,128)S(1)}, u32[]{:S(2)}, u32[]{:S(2)}) collective-permute-start(f32[2,512]{1,0:T(2,128)S(1)} %pad_maximum_fusion.3), channel_id=1, source_target_pairs={{0,2},{1,3},{2,0},{3,1},{4,6},{5,7},{6,4},{7,5},{8,10},{9,11},{10,... | collective-permute-start | bytes 12296 | tf_op jit(solution)/shard_map/ppermute | solution.py:37
  141.2 3.6 %collective-permute-start.28 = (f32[2,512]{1,0:T(2,128)S(1)}, f32[2,512]{1,0:T(2,128)S(1)}, u32[]{:S(2)}, u32[]{:S(2)}) collective-permute-start(f32[2,512]{1,0:T(2,128)S(1)} %pad_maximum_fusion.3), channel_id=1, source_target_pairs={{0,3},{1,0},{2,1},{3,2},{4,7},{5,4},{6,5},{7,6},{8,11},{9,8},{10,9... | collective-permute-start | bytes 12296 | tf_op jit(solution)/shard_map/ppermute | solution.py:37
  144.9 5.2 %collective-permute-start.29 = (f32[2,512]{1,0:T(2,128)S(1)}, f32[2,512]{1,0:T(2,128)S(1)}, u32[]{:S(2)}, u32[]{:S(2)}) collective-permute-start(f32[2,512]{1,0:T(2,128)S(1)} %pad_maximum_fusion.4), channel_id=1, source_target_pairs={{0,4},{4,0},{1,5},{5,1},{2,6},{6,2},{3,7},{7,3},{8,12},{12,8},{9,1... | collective-permute-start | bytes 12296 | tf_op jit(solution)/shard_map/ppermute | solution.py:37
